TPU v7x, 512 devices: a whole 4x8x8 slice. The times are simulated.
512 devices in a mesh: tok: 32 (over z_hi, y), exp: 16 (over z_lo, x, core).
Axes of the slice: x: 4, y: 8, z: 8 (z_hi: 4, z_lo: 2; z = z_hi * 2 + z_lo), core: 2. Of those that a mesh axis runs over, the one named last changes fastest.
Arguments:
- tokens: bfloat16 [8192, 4096], P('tok', 'exp'), may hold values from -6 to 6
- w_gate: bfloat16 [4096, 8192], P('tok', 'exp'), may hold values from -0.09375 to 0.09375
- w_up: bfloat16 [4096, 8192], P('tok', 'exp'), may hold values from -0.09375 to 0.09375
- w_down: bfloat16 [8192, 4096], P('exp', 'tok'), may hold values from -0.0625 to 0.0625
- pattern: int32 [64], P('tok'), may hold values from 0 to 1, as said below
- gate_code: int32 [8192], P('tok'), may hold values from 1 to 255
Outputs:
- moe_out: bfloat16 [8192, 4096], P('tok', 'exp')
Inputs may be any that keep to these rules, and one draw needn't show every extreme that they name: pattern holds 0 or 1 for each token block; in each aligned run of 2 blocks at most half are 1, and in every draw some run has exactly half.
All inputs are finite; a program needn't handle non-finite values.
Results may differ from a plain program's by a relative error of at most 0.0049.
Values may be sent and summed in bfloat16 or wider, within the bound.
No kernel may reach another device: no remote copies, remote signals or barrier semaphores. Data moves between devices by JAX's collectives and lax.ppermute only.
A program may use at most 64 MiB of HBM per device.

v0:
```python
import jax
import jax.numpy as jnp
from jax import lax
from jax.sharding import PartitionSpec as P


def per_device(tokens, w_gate, w_up, w_down, pattern, gate_code):
    row_count = tokens.shape[0]
    block_count = pattern.shape[0]
    block_rows = row_count // block_count
    flags = jnp.repeat(pattern, block_rows).astype(jnp.float32)
    row_scale = (gate_code.astype(jnp.float32) / 256.0 * flags).astype(jnp.bfloat16)
    active = [pattern[block_index] > 0 for block_index in range(block_count)]
    whole_rows = lax.all_gather(tokens, "exp", axis=1, tiled=True)
    col_count = w_gate.shape[1]
    empty = jnp.zeros((block_count, block_rows, col_count), jnp.float32)
    pieces = (
        lax.all_gather(w_gate, "tok", axis=0, tiled=True),
        lax.all_gather(w_up, "tok", axis=0, tiled=True),
    )
    gate_acc = empty
    up_acc = empty
    for block_index in range(block_count):
        rows_panel = whole_rows[block_index * block_rows : (block_index + 1) * block_rows]

        def add_block(pair, rows_panel=rows_panel):
            return (
                pair[0] + jnp.dot(rows_panel, pieces[0], preferred_element_type=jnp.float32),
                pair[1] + jnp.dot(rows_panel, pieces[1], preferred_element_type=jnp.float32),
            )

        def keep_pair(pair):
            return pair

        new_gate, new_up = lax.cond(
            active[block_index], add_block, keep_pair, (gate_acc[block_index], up_acc[block_index])
        )
        gate_acc = gate_acc.at[block_index].set(new_gate)
        up_acc = up_acc.at[block_index].set(new_up)
    hidden = (jax.nn.silu(gate_acc) * up_acc).astype(jnp.bfloat16)
    piece = lax.all_gather(w_down, "tok", axis=1, tiled=True)
    outputs = []
    for block_index in range(block_count):

        def busy_block(operand, block_index=block_index):
            return jnp.dot(hidden[block_index], operand, preferred_element_type=jnp.float32)

        def quiet_block(operand):
            return jnp.zeros((block_rows, operand.shape[1]), jnp.float32)

        outputs.append(lax.cond(active[block_index], busy_block, quiet_block, piece))
    partial_rows = jnp.concatenate(outputs, 0)
    summed = lax.psum_scatter(partial_rows, "exp", scatter_dimension=1, tiled=True)
    return (row_scale.astype(jnp.float32)[:, None] * summed).astype(jnp.bfloat16)


def solution(mesh):
    in_specs = (
        P("tok", "exp"),
        P("tok", "exp"),
        P("tok", "exp"),
        P("exp", "tok"),
        P("tok"),
        P("tok"),
    )
    out_specs = P("tok", "exp")
    return jax.shard_map(
        per_device, mesh=mesh, in_specs=in_specs, out_specs=out_specs, check_vma=False
    )
```

profile of v0, /device:TPU:6, one launch (start us, length us, event | category | flops | bytes accessed | tf_op | source)
XLA Modules:
  0.0 451.9 jit_solution(13286704982819716227)
XLA Ops:
  6.5 0.0 all-gather.5.cloned.1.call-start
  6.5 0.7 all-gather.5.cloned.1.call-update
  7.3 0.0 all-gather.7.cloned.1.call-start
  7.3 0.7 all-gather.7.cloned.1.call-update
  8.0 0.0 all-gather.9.cloned.1.call-start
  8.1 0.7 all-gather.9.cloned.1.call-update
  8.7 0.0 all-gather.11.cloned.1.call-start
  8.8 0.5 all-gather.11.cloned.1.call-update
  9.3 0.0 reduce-scatter.2.cloned.1.call-start
  9.4 1.4 fusion.13
  12.0 44.4 %all-gather.5.cloned.1.call-done = bf16[256,4096]{1,0:T(8,128)(2,1)} async-done(((bf16[256,256]{1,0:T(8,128)(2,1)}), bf16[256,4096]{1,0:T(8,128)(2,1)}) %all-gather.5.cloned.1.call-update) | async-done | bytes 2097168 | tf_op jit(solution)/shard_map/all_gather | solution.py:14
  56.4 106.7 %all-gather.7.cloned.1.call-done = bf16[4096,512]{1,0:T(8,128)(2,1)} async-done(((bf16[128,512]{1,0:T(8,128)(2,1)}), bf16[4096,512]{1,0:T(8,128)(2,1)}) %all-gather.7.cloned.1.call-update) | async-done | bytes 4194320 | tf_op jit(solution)/shard_map/all_gather | solution.py:18
  163.0 101.8 %all-gather.9.cloned.1.call-done = bf16[4096,512]{1,0:T(8,128)(2,1)} async-done(((bf16[128,512]{1,0:T(8,128)(2,1)}), bf16[4096,512]{1,0:T(8,128)(2,1)}) %all-gather.9.cloned.1.call-update) | async-done | bytes 4194320 | tf_op jit(solution)/shard_map/all_gather | solution.py:19
  264.9 5.8 %conditional.4 = (f32[1,128,512]{2,1,0:T(8,128)S(1)}, f32[1,128,512]{2,1,0:T(8,128)S(1)}) conditional(s32[]{:T(128)} %bitcast.5, () %tuple.67, (bf16[256,4096]{1,0:T(8,128)(2,1)}, bf16[4096,512]{1,0:T(8,128)(2,1)}, bf16[4096,512]{1,0:T(8,128)(2,1)}) %tuple.68), branch_computations={%region_0.0_spmd, %region_1.0_spmd} | conditional | flops 1073741824 | bytes 27787308 | solution.py:35
  264.9 0.0 copy-start.1
  264.9 3.4 convolution_bitcast_fusion
  268.3 0.4 copy-done.1
  268.7 2.0 convolution_bitcast_fusion.1
  270.7 0.1 fusion.10
  270.8 101.2 %all-gather.11.cloned.1.call-done = bf16[512,4096]{1,0:T(8,128)(2,1)} async-done(((bf16[512,128]{1,0:T(8,128)(2,1)}), bf16[512,4096]{1,0:T(8,128)(2,1)}) %all-gather.11.cloned.1.call-update) | async-done | bytes 4194320 | tf_op jit(solution)/shard_map/all_gather | solution.py:41
  372.0 2.9 conditional.6
  372.0 2.9 fusion.4
  375.0 1.6 conditional.7
  375.0 1.6 broadcast.82
  376.5 3.9 pad_maximum_fusion
  380.4 0.0 copy-start.2
  380.5 0.0 copy-start.3
  380.5 0.0 reduce-scatter.2.cloned.1.call-update
  380.5 0.6 copy-done.2
  381.1 0.0 copy-done.3
  381.1 0.1 fusion.12
  381.2 62.5 %reduce-scatter.2.cloned.1.call-done = f32[256,256]{1,0:T(8,128)} async-done(((f32[256,4096]{1,0:T(8,128)}), f32[256,256]{1,0:T(8,128)}) %reduce-scatter.2.cloned.1.call-update) | async-done | bytes 262160 | tf_op jit(solution)/shard_map/reduce_scatter | solution.py:53
  443.7 1.7 multiply_convert_fusion
  (4 shorter events, 0.1 us)
Async XLA Ops:
  6.5 49.8 %all-gather.5.cloned.1.call-start = ((), (), s32[]{:S(2)}) async-start(), calls=%async_computation.1 | async-start | bytes 2228224 | tf_op jit(solution)/shard_map/all_gather | solution.py:14
  7.3 155.8 %all-gather.7.cloned.1.call-start = ((), (), s32[]{:S(2)}) async-start(), calls=%async_computation.2 | async-start | bytes 4325376 | tf_op jit(solution)/shard_map/all_gather | solution.py:18
  8.0 256.8 %all-gather.9.cloned.1.call-start = ((), (), s32[]{:S(2)}) async-start(), calls=%async_computation.3 | async-start | bytes 4325376 | tf_op jit(solution)/shard_map/all_gather | solution.py:19
  8.7 363.3 %all-gather.11.cloned.1.call-start = ((), (), s32[]{:S(2)}) async-start(), calls=%async_computation.4 | async-start | bytes 4325376 | tf_op jit(solution)/shard_map/all_gather | solution.py:41
  9.3 434.4 %reduce-scatter.2.cloned.1.call-start = ((), (), s32[]{:S(2)}) async-start(), calls=%async_computation.5 | async-start | bytes 4456448 | tf_op jit(solution)/shard_map/reduce_scatter | solution.py:53
  264.9 3.7 copy-start.1
  380.4 0.7 copy-start.2
  380.5 0.7 copy-start.3
Sparse Core Ops, SparseCore 0:
  9.4 46.9 all-gather.4
  59.5 103.4 all-gather.6
  166.2 98.5 all-gather.8
  267.7 104.2 all-gather.10
  380.6 63.0 reduce-scatter.1
where the time goes:
time: 456 us; the launch traced here: 452 us
  waiting for transfers between devices  419 us (92%)
  between operations  14.5 us (3%)
  matrix products  8.26 us (2%)
  other arithmetic  5.85 us (1%)
    all_gather x1, waiting for transfers between devices, per_device(): lax.all_gather(w_gate, 'tok', axis=0, tiled=True)  107 us
    all_gather x1, waiting for transfers between devices, per_device(): lax.all_gather(w_up, 'tok', axis=0, tiled=True)  102 us
    all_gather x1, waiting for transfers between devices, per_device(): piece = lax.all_gather(w_down, 'tok', axis=1, tiled=True)  101 us
    reduce_scatter x1, waiting for transfers between devices, per_device(): lax.psum_scatter(partial_rows, 'exp', scatter_dimension=1, tiled=True)  62.5 us
    all_gather x1, waiting for transfers between devices, per_device(): whole_rows = lax.all_gather(tokens, 'exp', axis=1, tiled=True)  44.4 us
  transfers between devices with their start and end apart: 5, of which 5 were waited for; matrix products, arithmetic and copies ran while one was open for 2% of the time, Pallas kernels for 0%

commit v1 on v0

v1 whole, which is shorter than its diff:
```python
import jax
import jax.numpy as jnp
from jax import lax
from jax.sharding import Mesh
from jax.sharding import PartitionSpec as P

TOK = ("zh", "y")
EXP = ("zl", "x", "c")
F32, BF16 = jnp.float32, jnp.bfloat16


def per_device(tokens, w_gate, w_up, w_down, pattern, gate_code):
    zh = lax.axis_index("zh")
    core = lax.axis_index("c")
    row_count, width = tokens.shape
    block_count = pattern.shape[0]
    block_rows = row_count // block_count
    hidden_count = w_gate.shape[1]
    groups = lax.axis_size("zh")
    quarter = lax.axis_size(EXP) // groups

    both = lax.all_gather(jnp.concatenate([w_gate, w_up], 1), "y", axis=0, tiled=True)

    chosen = jnp.where(pattern[0] > 0, 0, 1)
    live = pattern[chosen] > 0
    rows = lax.dynamic_slice_in_dim(tokens, chosen * block_rows, block_rows, 0)
    codes = lax.dynamic_slice_in_dim(gate_code, chosen * block_rows, block_rows, 0)
    row_scale = (codes.astype(F32) / 256.0 * live.astype(F32)).astype(BF16)
    scale_rows = jnp.zeros((8, width), BF16).at[0, :block_rows].set(row_scale)
    carried = jnp.concatenate([rows, scale_rows], 0)

    size = lax.axis_size(EXP)
    swap = []
    for z in range(groups):
        for a in range(groups):
            for b in range(quarter):
                swap.append((z * size + a * quarter + b, a * size + z * quarter + b))
    carried = lax.ppermute(carried, ("zh",) + EXP, swap)
    scale = carried[block_rows, :block_rows].astype(F32)
    rows = carried[:block_rows]

    chips = lax.all_gather(rows, ("zl", "x"), axis=0, tiled=False)
    other = lax.ppermute(chips, "c", [(0, 1), (1, 0)])
    first = jnp.where(core == 0, chips, other)
    second = jnp.where(core == 0, other, chips)
    lhs = jnp.stack([first, second], 1).reshape(groups, quarter, block_rows, width)
    lhs = lhs.transpose(0, 2, 1, 3).reshape(groups * block_rows, quarter * width)

    down = lax.all_gather(w_down, "y", axis=1, tiled=True)

    product = jnp.dot(lhs, both, preferred_element_type=F32)
    sent = product.astype(BF16).reshape(groups, block_rows, 2 * hidden_count)
    got = lax.all_to_all(sent, "zh", split_axis=0, concat_axis=0, tiled=True)
    own = lax.dynamic_slice_in_dim(product, zh * block_rows, block_rows, 0)
    total = jnp.zeros_like(own)
    for k in range(groups):
        total = total + jnp.where(k == zh, own, got[k].astype(F32))
    hidden = (jax.nn.silu(total[:, :hidden_count]) * total[:, hidden_count:]).astype(BF16)

    hidden = lax.all_gather(hidden, "zh", axis=0, tiled=True)
    part = jnp.dot(hidden, down, preferred_element_type=F32).astype(BF16)
    part = part.reshape(groups, block_rows, quarter, width).transpose(0, 2, 1, 3)
    part = part.reshape(groups * quarter, block_rows, width)
    parts = lax.all_to_all(part, EXP, split_axis=0, concat_axis=0, tiled=True)
    summed = jnp.sum(parts.astype(F32), 0)
    result = (scale[:, None] * summed).astype(BF16)
    result = lax.ppermute(result, ("zh",) + EXP, swap)

    outs = []
    for block_index in range(block_count):
        keep = jnp.logical_and(chosen == block_index, live)
        outs.append(jnp.where(keep, result, jnp.zeros_like(result)))
    return jnp.concatenate(outs, 0)


def solution(mesh):
    wide = Mesh(mesh.devices.reshape(4, 8, 2, 4, 2), ("zh", "y", "zl", "x", "c"))
    in_specs = (
        P(TOK, EXP),
        P(TOK, EXP),
        P(TOK, EXP),
        P(EXP, TOK),
        P(TOK),
        P(TOK),
    )
    return jax.shard_map(
        per_device, mesh=wide, in_specs=in_specs, out_specs=P(TOK, EXP), check_vma=False
    )
```

time: 456 us -> 161 us (0.35)
  waiting for transfers between devices: 419 us -> 56 us
  blocking collectives: 0 us -> 47.4 us
  starting transfers between devices: 0.15 us -> 28.1 us
    all_gather x4 -> x2, waiting for transfers between devices: 354 us -> 4.47 us  [the longest x1 3.56 us: per_device(): down = lax.all_gather(w_down, 'y', axis=1, tiled=True)]
    reduce_scatter x1 -> x0, waiting for transfers between devices: 62.5 us -> none  [per_device(): lax.psum_scatter(partial_rows, 'exp', scatter_dimension=1, tiled=True)]
    all_gather x0 -> x2, blocking collectives: none -> 47.4 us  [the longest x1 30.7 us: per_device(): chips = lax.all_gather(rows, ('zl', 'x'), axis=0, tiled=False)]
    all_to_all x0 -> x2, waiting for transfers between devices: none -> 39.7 us  [the longest x1 24.8 us: per_device(): got = lax.all_to_all(sent, 'zh', split_axis=0, concat_axis=0, tiled=True)]
    all_to_all x0 -> x2, starting transfers between devices: none -> 15.1 us  [the longest x1 9.11 us: per_device(): got = lax.all_to_all(sent, 'zh', split_axis=0, concat_axis=0, tiled=True)]
    ppermute x0 -> x3, starting transfers between devices: none -> 13 us  [the longest x1 6.93 us: per_device(): carried = lax.ppermute(carried, ('zh',) + EXP, swap)]
    ppermute x0 -> x3, waiting for transfers between devices: none -> 11.2 us  [the longest x1 6.73 us: per_device(): result = lax.ppermute(result, ('zh',) + EXP, swap)]
  transfers between devices with their start and end apart: 5 -> 7, of which waited for: 5 -> 7; matrix products, arithmetic and copies ran while one was open for 2% -> 2% of each run, Pallas kernels for 0% -> 0%
where the time goes in v1:
time: 161 us; the launch traced here: 160 us
  waiting for transfers between devices  56 us (35%)
  blocking collectives  47.4 us (29%)
  starting transfers between devices  28.1 us (17%)
  between operations  14.9 us (9%)
  matrix products  5.79 us (4%)
  local copies, waits for them, and re-layouts  4.32 us (3%)
  other arithmetic  3.87 us (2%)
    all_gather x1, blocking collectives, per_device(): chips = lax.all_gather(rows, ('zl', 'x'), axis=0, tiled=False)  30.7 us
    all_to_all x1, waiting for transfers between devices, per_device(): got = lax.all_to_all(sent, 'zh', split_axis=0, concat_axis=0, tiled=True)  24.8 us
    all_gather x1, blocking collectives, per_device(): hidden = lax.all_gather(hidden, 'zh', axis=0, tiled=True)  16.7 us
    all_to_all x1, waiting for transfers between devices, per_device(): parts = lax.all_to_all(part, EXP, split_axis=0, concat_axis=0, tiled=True)  14.9 us
    all_to_all x1, starting transfers between devices, per_device(): got = lax.all_to_all(sent, 'zh', split_axis=0, concat_axis=0, tiled=True)  9.11 us
    ppermute x1, starting transfers between devices, per_device(): carried = lax.ppermute(carried, ('zh',) + EXP, swap)  6.93 us
    ppermute x1, waiting for transfers between devices, per_device(): result = lax.ppermute(result, ('zh',) + EXP, swap)  6.73 us
    all_to_all x1, starting transfers between devices, per_device(): parts = lax.all_to_all(part, EXP, split_axis=0, concat_axis=0, tiled=True)  6 us
  transfers between devices with their start and end apart: 7, of which 7 were waited for; matrix products, arithmetic and copies ran while one was open for 2% of the time, Pallas kernels for 0%

profile of v1, /device:TPU:6, one launch (start us, length us, event | category | flops | bytes accessed | tf_op | source)
XLA Modules:
  0.0 160.4 jit_solution(15437152779183797942)
XLA Ops:
  6.5 0.0 copy-start
  6.5 0.0 all-gather.4.cloned.1.call-start
  6.5 1.7 %pad_maximum_fusion.1 = bf16[128,1024]{1,0:T(8,128)(2,1)} fusion(bf16[128,512]{1,0:T(8,128)(2,1)} %param.10, bf16[128,512]{1,0:T(8,128)(2,1)} %param.9), kind=kLoop, calls=%fused_computation.18 | loop fusion | flops 524288 | bytes 524288 | tf_op jit(solution)/shard_map/concatenate | solution.py:22
  8.3 0.0 all-gather.4.cloned.1.call-update
  9.0 1.3 dynamic_slice.12
  11.0 0.8 convert_bitcast_fusion
  11.7 0.0 copy-done
  11.8 6.9 %collective-permute-start = (bf16[136,256]{1,0:T(8,128)(2,1)S(1)}, bf16[136,256]{1,0:T(8,128)(2,1)S(1)}, u32[]{:S(2)}, u32[]{:S(2)}) collective-permute-start(bf16[136,256]{1,0:T(8,128)(2,1)S(1)} %fusion.5), channel_id=1, source_target_pairs={{0,0},{1,1},{2,2},{3,3},{4,128},{5,129},{6,130},{7,131},{8,256},{9... | collective-permute-start | bytes 208904 | tf_op jit(solution)/shard_map/ppermute | solution.py:38
  18.7 2.6 %collective-permute-done = bf16[136,256]{1,0:T(8,128)(2,1)S(1)} collective-permute-done((bf16[136,256]{1,0:T(8,128)(2,1)S(1)}, bf16[136,256]{1,0:T(8,128)(2,1)S(1)}, u32[]{:S(2)}, u32[]{:S(2)}) %collective-permute-start) | collective-permute-done | bytes 69664 | tf_op jit(solution)/shard_map/ppermute | solution.py:38
  21.3 30.7 %all-gather = bf16[1024,256]{1,0:T(8,128)(2,1)S(1)} all-gather(bf16[128,256]{1,0:T(8,128)(2,1)S(1)} %slice.53), channel_id=2, replica_groups=mesh['zh'=4,'y'=8,'zl'=2,'x'=4,'c'=2] {'zl','x'}, dimensions={0}, use_global_device_ids=true | all-gather | bytes 589824 | tf_op jit(solution)/shard_map/all_gather | solution.py:42
  51.9 1.9 %collective-permute-start.1 = (bf16[8,128,256]{2,1,0:T(8,128)(2,1)S(1)}, bf16[8,128,256]{2,1,0:T(8,128)(2,1)S(1)}, u32[]{:S(2)}, u32[]{:S(2)}) collective-permute-start(bf16[8,128,256]{2,1,0:T(8,128)(2,1)S(1)} %bitcast.53), channel_id=1, source_target_pairs={{0,1},{1,0},{2,3},{3,2},{4,5},{5,4},{6,7},{7,6},{8,9},{9,8},{10,11... | collective-permute-start | bytes 1572872 | tf_op jit(solution)/shard_map/ppermute | solution.py:43
  53.9 1.9 %collective-permute-done.1 = bf16[8,128,256]{2,1,0:T(8,128)(2,1)S(1)} collective-permute-done((bf16[8,128,256]{2,1,0:T(8,128)(2,1)S(1)}, bf16[8,128,256]{2,1,0:T(8,128)(2,1)S(1)}, u32[]{:S(2)}, u32[]{:S(2)}) %collective-permute-start.1) | collective-permute-done | bytes 524320 | tf_op jit(solution)/shard_map/ppermute | solution.py:43
  55.7 0.1 select_bitcast_fusion.1
  55.8 0.1 pad_maximum_fusion
  55.9 0.8 copy.8
  56.7 0.2 copy.10
  57.0 0.9 all-gather.4.cloned.1.call-done
  57.9 3.8 %fusion.7 = (bf16[512,1024]{1,0:T(8,128)(2,1)}, f32[512,1024]{1,0:T(8,128)S(1)}) fusion(bf16[512,1024]{1,0:T(8,128)(2,1)S(1)} %bitcast.55, bf16[1024,1024]{1,0:T(8,128)(2,1)} %all-gather.4.cloned.1.call-done), kind=kOutput, calls=%fused_computation.30 | convolution fusion | flops 1074266112 | bytes 6291456 | tf_op jit(solution)/shard_map/dot_general | solution.py:51
  61.7 9.1 %all-to-all-start = ((bf16[4,128,1024]{2,1,0:T(8,128)(2,1)}), bf16[4,128,1024]{2,1,0:T(8,128)(2,1)S(1)}, u32[]{:S(2)}, u32[]{:S(2)}) async-start(bf16[4,128,1024]{2,1,0:T(8,128)(2,1)} %bitcast.10), calls=%async_computation | async-start | bytes 2097152 | tf_op jit(solution)/shard_map/all_to_all | solution.py:53
  70.8 0.0 all-gather.6.cloned.1.call-start
  70.8 0.7 all-gather.6.cloned.1.call-update
  71.5 24.8 %all-to-all-done = bf16[4,128,1024]{2,1,0:T(8,128)(2,1)S(1)} async-done(((bf16[4,128,1024]{2,1,0:T(8,128)(2,1)}), bf16[4,128,1024]{2,1,0:T(8,128)(2,1)S(1)}, u32[]{:S(2)}, u32[]{:S(2)}) %all-to-all-start) | async-done | bytes 1048608 | tf_op jit(solution)/shard_map/all_to_all | solution.py:53
  96.3 0.2 fusion
  96.5 0.1 fusion.3
  96.6 16.7 %all_gather.18 = bf16[512,512]{1,0:T(8,128)(2,1)S(1)} all-gather(bf16[128,512]{1,0:T(8,128)(2,1)S(1)} %fusion.3), channel_id=1, replica_groups=mesh['zh'=4,'y'=8,'zl'=2,'x'=4,'c'=2] {'zh'}, dimensions={0}, use_global_device_ids=true | all-gather | bytes 655360 | tf_op jit(solution)/shard_map/all_gather | solution.py:60
  113.3 3.6 %all-gather.6.cloned.1.call-done = bf16[512,1024]{1,0:T(8,128)(2,1)} async-done(((bf16[512,128]{1,0:T(8,128)(2,1)}), bf16[512,1024]{1,0:T(8,128)(2,1)}) %all-gather.6.cloned.1.call-update) | async-done | bytes 1048592 | tf_op jit(solution)/shard_map/all_gather | solution.py:49
  116.9 2.0 %convolution_convert_fusion = bf16[512,1024]{1,0:T(8,128)(2,1)S(1)} fusion(bf16[512,512]{1,0:T(8,128)(2,1)S(1)} %all_gather.18, bf16[512,1024]{1,0:T(8,128)(2,1)} %all-gather.6.cloned.1.call-done), kind=kOutput, calls=%fused_computation.1 | convolution fusion | flops 537395200 | bytes 2621440 | tf_op jit(solution)/shard_map/dot_general | solution.py:61
  118.9 0.8 reshape.71
  119.7 1.2 copy.9
  120.8 6.0 %all-to-all-start.1 = ((bf16[16,128,256]{2,1,0:T(8,128)(2,1)}), bf16[16,128,256]{2,1,0:T(8,128)(2,1)S(1)}, u32[]{:S(2)}, u32[]{:S(2)}) async-start(bf16[16,128,256]{2,1,0:T(8,128)(2,1)} %bitcast.16), calls=%async_computation.1 | async-start | bytes 2097152 | tf_op jit(solution)/shard_map/all_to_all | solution.py:64
  126.8 14.9 %all-to-all-done.1 = bf16[16,128,256]{2,1,0:T(8,128)(2,1)S(1)} async-done(((bf16[16,128,256]{2,1,0:T(8,128)(2,1)}), bf16[16,128,256]{2,1,0:T(8,128)(2,1)S(1)}, u32[]{:S(2)}, u32[]{:S(2)}) %all-to-all-start.1) | async-done | bytes 1048608 | tf_op jit(solution)/shard_map/all_to_all | solution.py:64
  141.7 0.1 convert_reduce_fusion
  141.9 0.1 multiply_convert_fusion
  142.0 4.1 %collective-permute-start.2 = (bf16[128,256]{1,0:T(8,128)(2,1)S(1)}, bf16[128,256]{1,0:T(8,128)(2,1)S(1)}, u32[]{:S(2)}, u32[]{:S(2)}) collective-permute-start(bf16[128,256]{1,0:T(8,128)(2,1)S(1)} %multiply_convert_fusion), channel_id=1, source_target_pairs={{0,0},{1,1},{2,2},{3,3},{4,128},{5,129},{6,130},{7,131},{8,256},{9... | collective-permute-start | bytes 196616 | tf_op jit(solution)/shard_map/ppermute | solution.py:67
  146.1 6.7 %collective-permute-done.2 = bf16[128,256]{1,0:T(8,128)(2,1)S(1)} collective-permute-done((bf16[128,256]{1,0:T(8,128)(2,1)S(1)}, bf16[128,256]{1,0:T(8,128)(2,1)S(1)}, u32[]{:S(2)}, u32[]{:S(2)}) %collective-permute-start.2) | collective-permute-done | bytes 65568 | tf_op jit(solution)/shard_map/ppermute | solution.py:67
  152.9 0.7 pad_maximum_fusion.2
  (5 shorter events, 0.0 us)
Async XLA Ops:
  6.5 5.2 %copy-start = (bf16[256,256]{1,0:T(8,128)(2,1)S(1)}, bf16[256,256]{1,0:T(8,128)(2,1)}, u32[]{:S(2)}) copy-start(bf16[256,256]{1,0:T(8,128)(2,1)} %param.8) | copy-start | bytes 393220
  6.5 51.3 %all-gather.4.cloned.1.call-start = ((), (), s32[]{:S(2)}) async-start(), calls=%async_computation.2 | async-start | bytes 2359296 | tf_op jit(solution)/shard_map/all_gather | solution.py:22
  11.8 9.5 %collective-permute-start = (bf16[136,256]{1,0:T(8,128)(2,1)S(1)}, bf16[136,256]{1,0:T(8,128)(2,1)S(1)}, u32[]{:S(2)}, u32[]{:S(2)}) collective-permute-start(bf16[136,256]{1,0:T(8,128)(2,1)S(1)} %fusion.5), channel_id=1, source_target_pairs={{0,0},{1,1},{2,2},{3,3},{4,128},{5,129},{6,130},{7,131},{8,256},{9... | collective-permute-start | bytes 208904 | tf_op jit(solution)/shard_map/ppermute | solution.py:38
  51.9 3.8 %collective-permute-start.1 = (bf16[8,128,256]{2,1,0:T(8,128)(2,1)S(1)}, bf16[8,128,256]{2,1,0:T(8,128)(2,1)S(1)}, u32[]{:S(2)}, u32[]{:S(2)}) collective-permute-start(bf16[8,128,256]{2,1,0:T(8,128)(2,1)S(1)} %bitcast.53), channel_id=1, source_target_pairs={{0,1},{1,0},{2,3},{3,2},{4,5},{5,4},{6,7},{7,6},{8,9},{9,8},{10,11... | collective-permute-start | bytes 1572872 | tf_op jit(solution)/shard_map/ppermute | solution.py:43
  61.7 34.6 %all-to-all-start = ((bf16[4,128,1024]{2,1,0:T(8,128)(2,1)}), bf16[4,128,1024]{2,1,0:T(8,128)(2,1)S(1)}, u32[]{:S(2)}, u32[]{:S(2)}) async-start(bf16[4,128,1024]{2,1,0:T(8,128)(2,1)} %bitcast.10), calls=%async_computation | async-start | bytes 2097152 | tf_op jit(solution)/shard_map/all_to_all | solution.py:53
  70.8 46.1 %all-gather.6.cloned.1.call-start = ((), (), s32[]{:S(2)}) async-start(), calls=%async_computation.3 | async-start | bytes 1179648 | tf_op jit(solution)/shard_map/all_gather | solution.py:49
  120.8 20.9 %all-to-all-start.1 = ((bf16[16,128,256]{2,1,0:T(8,128)(2,1)}), bf16[16,128,256]{2,1,0:T(8,128)(2,1)S(1)}, u32[]{:S(2)}, u32[]{:S(2)}) async-start(bf16[16,128,256]{2,1,0:T(8,128)(2,1)} %bitcast.16), calls=%async_computation.1 | async-start | bytes 2097152 | tf_op jit(solution)/shard_map/all_to_all | solution.py:64
  142.0 10.9 %collective-permute-start.2 = (bf16[128,256]{1,0:T(8,128)(2,1)S(1)}, bf16[128,256]{1,0:T(8,128)(2,1)S(1)}, u32[]{:S(2)}, u32[]{:S(2)}) collective-permute-start(bf16[128,256]{1,0:T(8,128)(2,1)S(1)} %multiply_convert_fusion), channel_id=1, source_target_pairs={{0,0},{1,1},{2,2},{3,3},{4,128},{5,129},{6,130},{7,131},{8,256},{9... | collective-permute-start | bytes 196616 | tf_op jit(solution)/shard_map/ppermute | solution.py:67
Sparse Core Ops, SparseCore 0:
  9.4 48.3 all-gather.3
  73.6 43.2 all-gather.5

commit v2 on v1

v2 whole, which is shorter than its diff:
```python
import jax
import jax.numpy as jnp
from jax import lax
from jax.experimental import pallas as pl
from jax.experimental.pallas import tpu as pltpu
from jax.sharding import Mesh
from jax.sharding import PartitionSpec as P

TOK = ("zh", "y")
EXP = ("zl", "x", "c")
F32, BF16 = jnp.float32, jnp.bfloat16
LANES = 128


def pack(w_gate, w_up, w_down):
    rows, cols = w_gate.shape
    panels = cols // LANES

    def body(gate_ref, up_ref, down_ref, out_ref):
        for j in range(panels):
            out_ref[j] = gate_ref[:, j * LANES : (j + 1) * LANES]
            out_ref[panels + j] = up_ref[:, j * LANES : (j + 1) * LANES]
            out_ref[2 * panels + j] = down_ref[j * rows : (j + 1) * rows]

    return pl.pallas_call(
        body,
        out_shape=jax.ShapeDtypeStruct((3 * panels, rows, LANES), BF16),
        name="pack",
    )(w_gate, w_up, w_down)


def first_product(where, mine, theirs, weights):
    groups, lows, rows, width = mine.shape
    ranks, panels, depth, _ = weights.shape
    used = panels // 3 * 2
    wide = 2 * LANES
    span = width // depth

    def body(where_ref, mine_ref, theirs_ref, w_ref, sent_ref, own_ref):
        acc = jnp.zeros((groups * rows, wide), F32)
        for low in range(lows):
            for flip, ref in enumerate((mine_ref, theirs_ref)):
                core = where_ref[1] if flip == 0 else 1 - where_ref[1]
                at = pl.ds((low * 2 + core) * span, span)
                rhs = jnp.concatenate([w_ref[at, i].reshape(width, LANES) for i in range(2)], 1)
                part = ref[:, low].reshape(groups * rows, width)
                acc = acc + jnp.dot(part, rhs, preferred_element_type=F32)
        sent_ref[...] = acc.astype(BF16).reshape(groups, rows, wide)
        for z in range(groups):

            @pl.when(where_ref[0] == z)
            def _(z=z):
                own_ref[...] = acc[z * rows : (z + 1) * rows]

    return pl.pallas_call(
        body,
        grid_spec=pltpu.PrefetchScalarGridSpec(
            num_scalar_prefetch=1,
            grid=(used // 2,),
            in_specs=[
                pl.BlockSpec(mine.shape, lambda j, s: (0, 0, 0, 0)),
                pl.BlockSpec(theirs.shape, lambda j, s: (0, 0, 0, 0)),
                pl.BlockSpec((ranks, 2, depth, LANES), lambda j, s: (0, j, 0, 0)),
            ],
            out_specs=[
                pl.BlockSpec((groups, rows, wide), lambda j, s: (0, 0, j)),
                pl.BlockSpec((rows, wide), lambda j, s: (0, j)),
            ],
        ),
        out_shape=[
            jax.ShapeDtypeStruct((groups, rows, used * LANES), BF16),
            jax.ShapeDtypeStruct((rows, used * LANES), F32),
        ],
        cost_estimate=pl.CostEstimate(
            flops=2 * groups * rows * ranks * depth * used * LANES, bytes_accessed=5 << 20, transcendentals=0
        ),
        name="first_product",
    )(where, mine, theirs, weights)


def second_product(where, hidden, near, far):
    rows, hidden_count = hidden.shape
    ranks, others = far.shape[:2]
    groups = others + 1
    panels = hidden_count // LANES

    def body(where_ref, hidden_ref, near_ref, far_ref, out_ref):
        value = hidden_ref[...]
        for s in range(groups):
            if s == 0:
                halves = [near_ref[i].reshape(hidden_count, LANES) for i in range(2)]
            else:
                halves = [far_ref[i, s - 1] for i in range(2)]
            part = jnp.dot(value, jnp.concatenate(halves, 1), preferred_element_type=F32)
            out_ref[lax.rem(where_ref[0] + s, groups), 0] = part.astype(BF16)

    return pl.pallas_call(
        body,
        grid_spec=pltpu.PrefetchScalarGridSpec(
            num_scalar_prefetch=1,
            grid=(ranks // 2,),
            in_specs=[
                pl.BlockSpec(hidden.shape, lambda j, s: (0, 0)),
                pl.BlockSpec((2, panels) + near.shape[2:], lambda j, s: (j, 2, 0, 0)),
                pl.BlockSpec((2,) + far.shape[1:], lambda j, s: (j, 0, 0, 0)),
            ],
            out_specs=pl.BlockSpec((groups, 1, rows, 2 * LANES), lambda j, s: (0, j, 0, 0)),
        ),
        out_shape=jax.ShapeDtypeStruct((groups, ranks // 2, rows, 2 * LANES), BF16),
        cost_estimate=pl.CostEstimate(
            flops=2 * rows * hidden_count * groups * ranks * LANES, bytes_accessed=5 << 20, transcendentals=0
        ),
        name="second_product",
    )(where, hidden, near, far)


def per_device(tokens, w_gate, w_up, w_down, pattern, gate_code):
    zh = lax.axis_index("zh")
    row_count, width = tokens.shape
    block_count = pattern.shape[0]
    block_rows = row_count // block_count
    groups, ranks, size = lax.axis_size("zh"), lax.axis_size("y"), lax.axis_size(EXP)
    quarter = size // groups
    where = jnp.stack([zh, lax.axis_index("c")]).astype(jnp.int32)

    near = lax.all_gather(pack(w_gate, w_up, w_down), "y", axis=0, tiled=False)
    columns = lax.all_gather(w_down, "zh", axis=0, tiled=False)
    others = jnp.stack([lax.dynamic_index_in_dim(columns, (zh + s) % groups, keepdims=False) for s in range(1, groups)])
    far = lax.all_gather(others, "y", axis=0, tiled=False)

    chosen = jnp.where(pattern[0] > 0, 0, 1)
    rows = lax.dynamic_slice_in_dim(tokens, chosen * block_rows, block_rows, 0)
    flags = jnp.repeat(pattern, block_rows).astype(F32)
    row_scale = (gate_code.astype(F32) / 256.0 * flags).astype(BF16).astype(F32)

    swap = []
    for z in range(groups):
        for a in range(groups):
            for b in range(quarter):
                swap.append((z * size + a * quarter + b, a * size + z * quarter + b))
    rows = lax.ppermute(rows, ("zh",) + EXP, swap)
    chips = size // 2
    copies = jnp.broadcast_to(rows[None], (chips,) + rows.shape)
    mine = lax.all_to_all(copies, ("zl", "x"), split_axis=0, concat_axis=0, tiled=True)
    mine = mine.reshape(groups, chips // groups, block_rows, width)
    theirs = lax.ppermute(mine, "c", [(0, 1), (1, 0)])

    sent, own = first_product(where, mine, theirs, near)
    got = lax.all_to_all(sent, "zh", split_axis=0, concat_axis=0, tiled=True)
    total = own
    for k in range(groups):
        total = total + jnp.where(k == zh, 0.0, got[k].astype(F32))
    gate, up = jnp.split(total, 2, 1)
    hidden = (jax.nn.silu(gate) * up).astype(BF16)

    part = second_product(where, hidden, near, far)
    parts = lax.all_to_all(part.reshape(size, block_rows, width), EXP, split_axis=0, concat_axis=0, tiled=True)
    summed = jnp.sum(parts.astype(F32), 0)
    result = row_scale.reshape(block_count, block_rows, 1) * summed[None]
    return result.astype(BF16).reshape(row_count, width)


def solution(mesh):
    wide = Mesh(mesh.devices.reshape(4, 8, 2, 4, 2), ("zh", "y", "zl", "x", "c"))
    in_specs = (
        P(TOK, EXP),
        P(TOK, EXP),
        P(TOK, EXP),
        P(EXP, TOK),
        P(TOK),
        P(TOK),
    )
    return jax.shard_map(
        per_device, mesh=wide, in_specs=in_specs, out_specs=P(TOK, EXP), check_vma=False
    )
```

time: 161 us -> 147 us (0.913); the launches traced: 160 us -> 144 us
  Pallas kernels: 0 us -> 12.9 us
  blocking collectives: 47.4 us -> 35.2 us
  starting transfers between devices: 28.1 us -> 21.3 us
  matrix products: 5.79 us -> 0 us
  local copies, waits for them, and re-layouts: 4.32 us -> 0.09 us
    all_gather x2 -> x1, blocking collectives: 47.4 us -> 21.9 us  [per_device(): columns = lax.all_gather(w_down, 'zh', axis=0, tiled=False)]
    all_to_all x0 -> x1, blocking collectives: none -> 13.3 us  [per_device(): lax.all_to_all(copies, ('zl', 'x'), split_axis=0, concat_axis=0, tiled=True)]
    pallas_call x0 -> x3, Pallas kernels: none -> 12.9 us  [the longest x1 5.61 us: first_product(): pl.pallas_call(body, grid_spec=pltpu.PrefetchScalarGridSpec(num_scalar_pr...]
    all_gather x2, waiting for transfers between devices: 4.47 us -> 11.3 us  [the longest x1 8.51 us: per_device(): far = lax.all_gather(others, 'y', axis=0, tiled=False)]
    ppermute x3 -> x2, waiting for transfers between devices: 11.2 us -> 5.27 us  [the longest x1 4.04 us: per_device(): rows = lax.ppermute(rows, ('zh',) + EXP, swap)]
    dot_general x2 -> x0, matrix products: 5.79 us -> none  [the longest x1 3.83 us: per_device(): product = jnp.dot(lhs, both, preferred_element_type=F32)]
    ppermute x3 -> x2, starting transfers between devices: 13 us -> 8.03 us  [the longest x1 6.12 us: per_device(): rows = lax.ppermute(rows, ('zh',) + EXP, swap)]
    concatenate x3 -> x0, other arithmetic: 2.41 us -> none  [the longest x1 1.74 us: per_device(): jnp.concatenate([w_gate, w_up], 1)]
  transfers between devices with their start and end apart: 7 -> 6, of which waited for: 7 -> 6; matrix products, arithmetic and copies ran while one was open for 2% -> 3% of each run, Pallas kernels for 0% -> 4%
where the time goes in v2:
time: 147 us; the launch traced here: 144 us
  waiting for transfers between devices  56.5 us (38%)
  blocking collectives  35.2 us (24%)
  starting transfers between devices  21.3 us (14%)
  between operations  13.6 us (9%)
  Pallas kernels  12.9 us (9%)
  other arithmetic  4.43 us (3%)
    all_to_all x1, waiting for transfers between devices, per_device(): got = lax.all_to_all(sent, 'zh', split_axis=0, concat_axis=0, tiled=True)  25 us
    all_gather x1, blocking collectives, per_device(): columns = lax.all_gather(w_down, 'zh', axis=0, tiled=False)  21.9 us
    all_to_all x1, waiting for transfers between devices, per_device(): lax.all_to_all(part.reshape(size, block_rows, width), EXP, split_axis=0,...  14.8 us
    all_to_all x1, blocking collectives, per_device(): lax.all_to_all(copies, ('zl', 'x'), split_axis=0, concat_axis=0, tiled=True)  13.3 us
    all_gather x1, waiting for transfers between devices, per_device(): far = lax.all_gather(others, 'y', axis=0, tiled=False)  8.51 us
    all_to_all x1, starting transfers between devices, per_device(): got = lax.all_to_all(sent, 'zh', split_axis=0, concat_axis=0, tiled=True)  7.38 us
    ppermute x1, starting transfers between devices, per_device(): rows = lax.ppermute(rows, ('zh',) + EXP, swap)  6.12 us
    all_to_all x1, starting transfers between devices, per_device(): lax.all_to_all(part.reshape(size, block_rows, width), EXP, split_axis=0,...  5.89 us
  transfers between devices with their start and end apart: 6, of which 6 were waited for; matrix products, arithmetic and copies ran while one was open for 3% of the time, Pallas kernels for 4%

profile of v2, /device:TPU:6, one launch (start us, length us, event | category | flops | bytes accessed | tf_op | source)
XLA Modules:
  0.0 144.0 jit_solution(1278723353274972527)
XLA Ops:
  6.5 0.0 copy-start
  6.5 0.0 copy-start.4
  6.5 0.0 all-gather.6.cloned.1.call-start
  6.5 1.9 %pack.1 = bf16[12,128,128]{2,1,0:T(8,128)(2,1)} custom-call(bf16[128,512]{1,0:T(8,128)(2,1)} %gate_ref.1, bf16[128,512]{1,0:T(8,128)(2,1)} %up_ref.1, bf16[512,128]{1,0:T(8,128)(2,1)} %down_ref.1), custom_call_target="tpu_custom_call" | custom-call | tf_op jit(solution)/shard_map/pack/pallas_call | solution.py:25
  8.4 0.0 all-gather.6.cloned.1.call-update
  8.5 0.0 all-gather.8.cloned.1.call-start
  8.5 21.9 %all-gather.1 = bf16[2048,128]{1,0:T(8,128)(2,1)S(1)} all-gather(bf16[512,128]{1,0:T(8,128)(2,1)} %down_ref.1), channel_id=3, replica_groups=mesh['zh'=4,'y'=8,'zl'=2,'x'=4,'c'=2] {'zh'}, dimensions={0}, use_global_device_ids=true | all-gather | bytes 655360 | tf_op jit(solution)/shard_map/all_gather | solution.py:127
  30.5 0.8 pad_maximum_fusion
  31.3 0.0 all-gather.8.cloned.1.call-update
  31.4 0.0 copy-done.4
  31.4 0.0 copy-done
  31.4 6.1 %collective-permute-start = (bf16[128,256]{1,0:T(8,128)(2,1)S(1)}, bf16[128,256]{1,0:T(8,128)(2,1)S(1)}, u32[]{:S(2)}, u32[]{:S(2)}) collective-permute-start(bf16[128,256]{1,0:T(8,128)(2,1)S(1)} %constant_dynamic-slice_fusion.3), channel_id=1, source_target_pairs={{0,0},{1,1},{2,2},{3,3},{4,128},{5,129},{6,130},{7,131},{8,256},{9... | collective-permute-start | bytes 196616 | tf_op jit(solution)/shard_map/ppermute | solution.py:141
  37.6 4.0 %collective-permute-done = bf16[128,256]{1,0:T(8,128)(2,1)S(1)} collective-permute-done((bf16[128,256]{1,0:T(8,128)(2,1)S(1)}, bf16[128,256]{1,0:T(8,128)(2,1)S(1)}, u32[]{:S(2)}, u32[]{:S(2)}) %collective-permute-start) | collective-permute-done | bytes 65568 | tf_op jit(solution)/shard_map/ppermute | solution.py:141
  41.6 13.3 %all_to_all.15 = bf16[8,128,256]{2,1,0:T(8,128)(2,1)S(1)} all-to-all(bf16[8,128,256]{2,1,0:T(8,128)(2,1)S(1)} %broadcast_in_dim.18), channel_id=1, replica_groups=mesh['zh'=4,'y'=8,'zl'=2,'x'=4,'c'=2] {'zl','x'}, dimensions={0} | all-to-all | bytes 1048576 | tf_op jit(solution)/shard_map/all_to_all | solution.py:144
  54.9 0.0 copy-start.1
  54.9 1.9 %collective-permute-start.1 = (bf16[4,2,128,256]{3,2,1,0:T(8,128)(2,1)S(1)}, bf16[4,2,128,256]{3,2,1,0:T(8,128)(2,1)S(1)}, u32[]{:S(2)}, u32[]{:S(2)}) collective-permute-start(bf16[4,2,128,256]{3,2,1,0:T(8,128)(2,1)S(1)} %bitcast.37), channel_id=1, source_target_pairs={{0,1},{1,0},{2,3},{3,2},{4,5},{5,4},{6,7},{7,6},{8,9},{9,8},{10,11... | collective-permute-start | bytes 1572872 | tf_op jit(solution)/shard_map/ppermute | solution.py:146
  56.9 0.6 pad_add_fusion.where_ref
  57.5 1.2 collective-permute-done.1.theirs_ref
  58.7 0.0 copy-start.2
  58.7 2.8 %all-gather.6.cloned.1.call-done = bf16[96,128,128]{2,1,0:T(8,128)(2,1)} async-done(((bf16[12,128,128]{2,1,0:T(8,128)(2,1)}), bf16[96,128,128]{2,1,0:T(8,128)(2,1)}) %all-gather.6.cloned.1.call-update) | async-done | bytes 3145744 | tf_op jit(solution)/shard_map/all_gather | solution.py:126
  61.5 0.0 copy-done.1
  61.5 0.0 copy-done.2
  61.5 5.6 %first_product.1 = (bf16[4,128,1024]{2,1,0:T(8,128)(2,1)}, f32[128,1024]{1,0:T(8,128)}) custom-call(s32[2]{0:T(128)} %pad_add_fusion.where_ref, bf16[4,2,128,256]{3,2,1,0:T(8,128)(2,1)} %bitcast.38, bf16[4,2,128,256]{3,2,1,0:T(8,128)(2,1)} %copy-done.2, bf16[8,12,128,128]{3,2,1,0:T(8,128)(2,1)} %bitcast.33), custom_call_target="tpu_custom_call" | custom-call | flops 1073741824 | bytes 5242880 | tf_op jit(solution)/shard_map/first_product/pallas_call | solution.py:55
  67.1 7.4 %all-to-all-start.1 = ((bf16[4,128,1024]{2,1,0:T(8,128)(2,1)}), bf16[4,128,1024]{2,1,0:T(8,128)(2,1)S(1)}, u32[]{:S(2)}, u32[]{:S(2)}) async-start(bf16[4,128,1024]{2,1,0:T(8,128)(2,1)} %get-tuple-element.8), calls=%async_computation.1 | async-start | bytes 2097152 | tf_op jit(solution)/shard_map/all_to_all | solution.py:149
  74.5 25.0 %all-to-all-done.1 = bf16[4,128,1024]{2,1,0:T(8,128)(2,1)S(1)} async-done(((bf16[4,128,1024]{2,1,0:T(8,128)(2,1)}), bf16[4,128,1024]{2,1,0:T(8,128)(2,1)S(1)}, u32[]{:S(2)}, u32[]{:S(2)}) %all-to-all-start.1) | async-done | bytes 1048608 | tf_op jit(solution)/shard_map/all_to_all | solution.py:149
  99.5 1.3 bitcast_add_fusion
  100.8 0.7 fusion.hidden_ref
  101.5 8.5 %all-gather.8.cloned.1.call-done = bf16[24,512,128]{2,1,0:T(8,128)(2,1)} async-done(((bf16[3,512,128]{2,1,0:T(8,128)(2,1)}), bf16[24,512,128]{2,1,0:T(8,128)(2,1)}) %all-gather.8.cloned.1.call-update) | async-done | bytes 3145744 | tf_op jit(solution)/shard_map/all_gather | solution.py:129
  110.1 0.0 copy-start.3
  110.1 5.4 %second_product.1 = bf16[4,4,128,256]{3,2,1,0:T(8,128)(2,1)} custom-call(s32[2]{0:T(128)} %pad_add_fusion.where_ref, bf16[128,512]{1,0:T(8,128)(2,1)} %fusion.hidden_ref, bf16[8,12,128,128]{3,2,1,0:T(8,128)(2,1)} %bitcast.34, bf16[8,3,512,128]{3,2,1,0:T(8,128)(2,1)} %bitcast.36), custom_call_target="tpu_custom_call" | custom-call | flops 536870912 | bytes 5242880 | tf_op jit(solution)/shard_map/second_product/pallas_call | solution.py:97
  115.4 5.9 %all-to-all-start.2 = ((bf16[16,128,256]{2,1,0:T(8,128)(2,1)}), bf16[16,128,256]{2,1,0:T(8,128)(2,1)S(1)}, u32[]{:S(2)}, u32[]{:S(2)}) async-start(bf16[16,128,256]{2,1,0:T(8,128)(2,1)} %bitcast.35), calls=%async_computation.2 | async-start | bytes 2097152 | tf_op jit(solution)/shard_map/all_to_all | solution.py:157
  121.3 0.0 copy-done.3
  121.3 0.1 fusion.3
  121.4 14.8 %all-to-all-done.2 = bf16[16,128,256]{2,1,0:T(8,128)(2,1)S(1)} async-done(((bf16[16,128,256]{2,1,0:T(8,128)(2,1)}), bf16[16,128,256]{2,1,0:T(8,128)(2,1)S(1)}, u32[]{:S(2)}, u32[]{:S(2)}) %all-to-all-start.2) | async-done | bytes 1048608 | tf_op jit(solution)/shard_map/all_to_all | solution.py:157
  136.2 0.1 convert_reduce_fusion
  136.4 0.8 fusion.1
  (4 shorter events, 0.1 us)
Async XLA Ops:
  6.5 24.9 %copy-start = (bf16[256,256]{1,0:T(8,128)(2,1)S(1)}, bf16[256,256]{1,0:T(8,128)(2,1)}, u32[]{:S(2)}) copy-start(bf16[256,256]{1,0:T(8,128)(2,1)} %param.6) | copy-start | bytes 393220
  6.5 24.8 %copy-start.4 = (s32[2]{0:T(128)S(1)}, s32[2]{0:T(128)}, u32[]{:S(2)}) copy-start(s32[2]{0:T(128)} %param.10) | copy-start | bytes 28
  6.5 55.0 %all-gather.6.cloned.1.call-start = ((), (), s32[]{:S(2)}) async-start(), calls=%async_computation.3 | async-start | bytes 3538944 | tf_op jit(solution)/shard_map/all_gather | solution.py:126
  8.5 101.6 %all-gather.8.cloned.1.call-start = ((), (), s32[]{:S(2)}) async-start(), calls=%async_computation.4 | async-start | bytes 3538944 | tf_op jit(solution)/shard_map/all_gather | solution.py:129
  31.4 10.2 %collective-permute-start = (bf16[128,256]{1,0:T(8,128)(2,1)S(1)}, bf16[128,256]{1,0:T(8,128)(2,1)S(1)}, u32[]{:S(2)}, u32[]{:S(2)}) collective-permute-start(bf16[128,256]{1,0:T(8,128)(2,1)S(1)} %constant_dynamic-slice_fusion.3), channel_id=1, source_target_pairs={{0,0},{1,1},{2,2},{3,3},{4,128},{5,129},{6,130},{7,131},{8,256},{9... | collective-permute-start | bytes 196616 | tf_op jit(solution)/shard_map/ppermute | solution.py:141
  54.9 6.6 %copy-start.1 = (bf16[8,128,256]{2,1,0:T(8,128)(2,1)}, bf16[8,128,256]{2,1,0:T(8,128)(2,1)S(1)}, u32[]{:S(2)}) copy-start(bf16[8,128,256]{2,1,0:T(8,128)(2,1)S(1)} %all_to_all.15) | copy-start | bytes 1572868
  54.9 3.8 %collective-permute-start.1 = (bf16[4,2,128,256]{3,2,1,0:T(8,128)(2,1)S(1)}, bf16[4,2,128,256]{3,2,1,0:T(8,128)(2,1)S(1)}, u32[]{:S(2)}, u32[]{:S(2)}) collective-permute-start(bf16[4,2,128,256]{3,2,1,0:T(8,128)(2,1)S(1)} %bitcast.37), channel_id=1, source_target_pairs={{0,1},{1,0},{2,3},{3,2},{4,5},{5,4},{6,7},{7,6},{8,9},{9,8},{10,11... | collective-permute-start | bytes 1572872 | tf_op jit(solution)/shard_map/ppermute | solution.py:146
  58.7 2.8 %copy-start.2 = (bf16[4,2,128,256]{3,2,1,0:T(8,128)(2,1)}, bf16[4,2,128,256]{3,2,1,0:T(8,128)(2,1)S(1)}, u32[]{:S(2)}) copy-start(bf16[4,2,128,256]{3,2,1,0:T(8,128)(2,1)S(1)} %collective-permute-done.1.theirs_ref) | copy-start | bytes 1572868
  67.1 32.4 %all-to-all-start.1 = ((bf16[4,128,1024]{2,1,0:T(8,128)(2,1)}), bf16[4,128,1024]{2,1,0:T(8,128)(2,1)S(1)}, u32[]{:S(2)}, u32[]{:S(2)}) async-start(bf16[4,128,1024]{2,1,0:T(8,128)(2,1)} %get-tuple-element.8), calls=%async_computation.1 | async-start | bytes 2097152 | tf_op jit(solution)/shard_map/all_to_all | solution.py:149
  110.1 11.3 %copy-start.3 = (s32[256]{0:T(256)S(1)}, s32[256]{0:T(256)}, u32[]{:S(2)}) copy-start(s32[256]{0:T(256)} %param.11) | copy-start | bytes 3076
  115.4 20.8 %all-to-all-start.2 = ((bf16[16,128,256]{2,1,0:T(8,128)(2,1)}), bf16[16,128,256]{2,1,0:T(8,128)(2,1)S(1)}, u32[]{:S(2)}, u32[]{:S(2)}) async-start(bf16[16,128,256]{2,1,0:T(8,128)(2,1)} %bitcast.35), calls=%async_computation.2 | async-start | bytes 2097152 | tf_op jit(solution)/shard_map/all_to_all | solution.py:157
Sparse Core Ops, SparseCore 0:
  9.4 52.0 all-gather.5
  63.6 46.4 all-gather.7

commit v3 on v2

v3 whole, which is shorter than its diff:
```python
import jax
import jax.numpy as jnp
from jax import lax
from jax.experimental import pallas as pl
from jax.experimental.pallas import tpu as pltpu
from jax.sharding import Mesh
from jax.sharding import PartitionSpec as P

TOK = ("zh", "y")
EXP = ("zl", "x", "c")
F32, BF16 = jnp.float32, jnp.bfloat16
LANES = 128


def first_product(where, mine, theirs, weights):
    groups, lows, rows, width = mine.shape
    depth, cols = weights.shape
    wide = 2 * LANES

    def body(where_ref, mine_ref, theirs_ref, w_ref, sent_ref, own_ref):
        acc = jnp.zeros((groups * rows, wide), F32)
        for low in range(lows):
            for flip, ref in enumerate((mine_ref, theirs_ref)):
                core = where_ref[1] if flip == 0 else 1 - where_ref[1]
                at = pl.ds(pl.multiple_of((low * 2 + core) * width, width), width)
                part = ref[:, low].reshape(groups * rows, width)
                acc = acc + jnp.dot(part, w_ref[at, :], preferred_element_type=F32)
        sent_ref[...] = acc.astype(BF16).reshape(groups, rows, wide)
        for z in range(groups):

            @pl.when(where_ref[0] == z)
            def _(z=z):
                own_ref[...] = acc[z * rows : (z + 1) * rows]

    return pl.pallas_call(
        body,
        grid_spec=pltpu.PrefetchScalarGridSpec(
            num_scalar_prefetch=1,
            grid=(cols // wide,),
            in_specs=[
                pl.BlockSpec(mine.shape, lambda j, s: (0, 0, 0, 0)),
                pl.BlockSpec(theirs.shape, lambda j, s: (0, 0, 0, 0)),
                pl.BlockSpec((depth, wide), lambda j, s: (0, j)),
            ],
            out_specs=[
                pl.BlockSpec((groups, rows, wide), lambda j, s: (0, 0, j)),
                pl.BlockSpec((rows, wide), lambda j, s: (0, j)),
            ],
        ),
        out_shape=[
            jax.ShapeDtypeStruct((groups, rows, cols), BF16),
            jax.ShapeDtypeStruct((rows, cols), F32),
        ],
        cost_estimate=pl.CostEstimate(
            flops=2 * groups * rows * depth * cols, bytes_accessed=5 << 20, transcendentals=0
        ),
        name="first_product",
    )(where, mine, theirs, weights)


def second_product(where, mine, theirs, down):
    rows, depth = mine[0].shape
    ranks, kinds = down.shape[:2]
    width = 2 * LANES

    def body(where_ref, a_ref, b_ref, c_ref, d_ref, down_ref, out_ref):
        core = where_ref[1]
        kind = jnp.where(where_ref[0] // 2 == core, 0, 1)
        left = jnp.concatenate([a_ref[...], b_ref[...]], 0)
        right = jnp.concatenate([c_ref[...], d_ref[...]], 0)
        part = jnp.dot(left, jnp.concatenate([down_ref[i, kind] for i in range(2)], 1), preferred_element_type=F32)
        part = part + jnp.dot(
            right, jnp.concatenate([down_ref[i, 1 - kind] for i in range(2)], 1), preferred_element_type=F32
        )
        out_ref[core, 0] = part[:rows].astype(BF16)
        out_ref[1 - core, 0] = part[rows:].astype(BF16)

    return pl.pallas_call(
        body,
        grid_spec=pltpu.PrefetchScalarGridSpec(
            num_scalar_prefetch=1,
            grid=(ranks // 2,),
            in_specs=[pl.BlockSpec((rows, depth), lambda j, s: (0, 0))] * 4
            + [pl.BlockSpec((2,) + down.shape[1:], lambda j, s: (j, 0, 0, 0))],
            out_specs=pl.BlockSpec((2, 1, rows, width), lambda j, s: (0, j % 2 * 2 + j // 2, 0, 0)),
        ),
        out_shape=jax.ShapeDtypeStruct((2, ranks // 2, rows, width), BF16),
        cost_estimate=pl.CostEstimate(
            flops=2 * 2 * rows * depth * kinds * ranks * LANES, bytes_accessed=4 << 20, transcendentals=0
        ),
        name="second_product",
    )(where, *mine, *theirs, down)


def per_device(tokens, w_gate, w_up, w_down, pattern, gate_code):
    zh = lax.axis_index("zh")
    row_count, width = tokens.shape
    block_count = pattern.shape[0]
    block_rows = row_count // block_count
    groups, size = lax.axis_size("zh"), lax.axis_size(EXP)
    quarter = size // groups
    where = jnp.stack([zh, lax.axis_index("c")]).astype(jnp.int32)

    both = lax.all_gather(jnp.concatenate([w_gate, w_up], 1), "y", axis=0, tiled=True)
    blocks = []
    for flip in range(2):
        moves = []
        for z in range(groups):
            for c in range(2):
                moves.append(((z % 2 + 2 * c) * 2 + (z // 2 + flip) % 2, z * 2 + c))
        blocks.append(lax.ppermute(w_down, ("zh", "c"), moves))
    down = lax.all_gather(jnp.stack(blocks), "y", axis=0, tiled=False)

    chosen = jnp.where(pattern[0] > 0, 0, 1)
    rows = lax.dynamic_slice_in_dim(tokens, chosen * block_rows, block_rows, 0)
    codes = lax.dynamic_slice_in_dim(gate_code, chosen * block_rows, block_rows, 0)
    live = pattern[chosen] > 0
    row_scale = (codes.astype(F32) / 256.0 * live.astype(F32)).astype(BF16)
    neighbour = [(i, i ^ 1) for i in range(groups)]
    swap = []
    for z in range(groups):
        for a in range(groups):
            for b in range(quarter):
                swap.append((z * size + a * quarter + b, a * size + z * quarter + b))
    rows = lax.ppermute(rows, ("zh",) + EXP, swap)
    chips = size // 2
    copies = jnp.broadcast_to(rows[None], (chips,) + rows.shape)
    mine = lax.all_to_all(copies, ("zl", "x"), split_axis=0, concat_axis=0, tiled=True)
    mine = mine.reshape(groups, chips // groups, block_rows, width)
    theirs = lax.ppermute(mine, "c", [(0, 1), (1, 0)])

    sent, own = first_product(where, mine, theirs, both)
    got = lax.all_to_all(sent, "zh", split_axis=0, concat_axis=0, tiled=True)
    total = own
    for k in range(groups):
        total = total + jnp.where(k == zh, 0.0, got[k].astype(F32))
    gate, up = jnp.split(total, 2, 1)
    hidden = (jax.nn.silu(gate) * up).astype(BF16)

    cores = [(0, 1), (1, 0)]
    row_scale, own = lax.optimization_barrier((row_scale, own))
    passed = lax.ppermute(row_scale, "zh", neighbour)
    hidden, row_scale, passed = lax.optimization_barrier((hidden, row_scale, passed))
    scale = jnp.where(lax.axis_index("zl") == lax.axis_index("c"), row_scale, passed)

    beside = lax.ppermute(hidden, "zh", neighbour)
    mine = (hidden, beside)
    theirs = (lax.ppermute(hidden, "c", cores), lax.ppermute(beside, "c", cores))
    part = second_product(where, mine, theirs, down)
    parts = lax.all_to_all(part.reshape(chips, block_rows, width), ("zl", "x"), split_axis=0, concat_axis=0, tiled=True)
    summed = jnp.sum(parts.astype(F32), 0)
    result = (scale.astype(F32)[:, None] * summed).astype(BF16)
    home = []
    for z in range(groups):
        for zl in range(2):
            for high in range(2):
                for low in range(2):
                    for c in range(2):
                        source = z * size + zl * 8 + (high * 2 + low) * 2 + c
                        target = z if zl == c else z ^ 1
                        home.append((source, target * size + c * 8 + (z % 2 * 2 + low) * 2 + high))
    result = lax.ppermute(result, ("zh",) + EXP, home)

    outs = []
    for block_index in range(block_count):
        keep = jnp.logical_and(chosen == block_index, live)
        outs.append(jnp.where(keep, result, jnp.zeros_like(result)))
    return jnp.concatenate(outs, 0)


def solution(mesh):
    wide = Mesh(mesh.devices.reshape(4, 8, 2, 4, 2), ("zh", "y", "zl", "x", "c"))
    in_specs = (
        P(TOK, EXP),
        P(TOK, EXP),
        P(TOK, EXP),
        P(EXP, TOK),
        P(TOK),
        P(TOK),
    )
    return jax.shard_map(
        per_device, mesh=wide, in_specs=in_specs, out_specs=P(TOK, EXP), check_vma=False
    )
```

time: 147 us -> 143 us (0.973); the launches traced: 144 us -> 143 us
  blocking collectives: 35.2 us -> 0 us
  starting transfers between devices: 21.3 us -> 51.9 us
  Pallas kernels: 12.9 us -> 10.5 us
  waiting for transfers between devices: 56.5 us -> 58.8 us
  local copies, waits for them, and re-layouts: 0.09 us -> 2.22 us
    ppermute x0 -> x7, starting transfers between devices: none -> 22.2 us  [the longest x2 7.96 us: per_device(): blocks.append(lax.ppermute(w_down, ('zh', 'c'), moves))]
    all_gather x1 -> x0, blocking collectives: 21.9 us -> none  [per_device(): columns = lax.all_gather(w_down, 'zh', axis=0, tiled=False)]
    all_to_all x1 -> x0, blocking collectives: 13.3 us -> none  [per_device(): lax.all_to_all(copies, ('zl', 'x'), split_axis=0, concat_axis=0, tiled=True)]
    ppermute x0 -> x7, waiting for transfers between devices: none -> 11.9 us  [the longest x1 7.93 us: per_device(): result = lax.ppermute(result, ('zh',) + EXP, home)]
    all_to_all x1, waiting for transfers between devices: 25 us -> 17.9 us  [per_device(): got = lax.all_to_all(sent, 'zh', split_axis=0, concat_axis=0, tiled=True)]
    all_to_all x1 -> x2, starting transfers between devices: 5.89 us -> 12.9 us  [the longest x1 8.15 us: per_device(): lax.all_to_all(copies, ('zl', 'x'), split_axis=0, concat_axis=0, tiled=True)]
    ppermute x1, waiting for transfers between devices: 4.04 us -> 0.01 us  [per_device(): rows = lax.ppermute(rows, ('zh',) + EXP, swap)]
    concatenate x0 -> x2, other arithmetic: none -> 2.4 us  [the longest x1 1.73 us: per_device(): jnp.concatenate([w_gate, w_up], 1)]
  transfers between devices with their start and end apart: 6 -> 14, of which waited for: 6 -> 8; matrix products, arithmetic and copies ran while one was open for 3% -> 2% of each run, Pallas kernels for 4% -> 4%
where the time goes in v3:
time: 143 us
  waiting for transfers between devices  58.8 us (41%)
  starting transfers between devices  51.9 us (36%)
  between operations  14.9 us (10%)
  Pallas kernels  10.5 us (7%)
  other arithmetic  4.34 us (3%)
  local copies, waits for them, and re-layouts  2.22 us (2%)
    all_to_all x1, waiting for transfers between devices, per_device(): got = lax.all_to_all(sent, 'zh', split_axis=0, concat_axis=0, tiled=True)  17.9 us
    all_gather x1, waiting for transfers between devices, per_device(): lax.all_gather(jnp.concatenate([w_gate, w_up], 1), 'y', axis=0, tiled=True)  12.7 us
    all_to_all x1, starting transfers between devices, per_device(): lax.all_to_all(copies, ('zl', 'x'), split_axis=0, concat_axis=0, tiled=True)  8.15 us
    ppermute x2, starting transfers between devices, per_device(): blocks.append(lax.ppermute(w_down, ('zh', 'c'), moves))  7.96 us
    ppermute x1, waiting for transfers between devices, per_device(): result = lax.ppermute(result, ('zh',) + EXP, home)  7.93 us
    all_to_all x1, starting transfers between devices, per_device(): got = lax.all_to_all(sent, 'zh', split_axis=0, concat_axis=0, tiled=True)  7.91 us
    all_to_all x1, waiting for transfers between devices, per_device(): lax.all_to_all(part.reshape(chips, block_rows, width), ('zl', 'x'), split...  7.77 us
    all_to_all x1, waiting for transfers between devices, per_device(): lax.all_to_all(copies, ('zl', 'x'), split_axis=0, concat_axis=0, tiled=True)  7.32 us
  transfers between devices with their start and end apart: 14, of which 8 were waited for; matrix products, arithmetic and copies ran while one was open for 2% of the time, Pallas kernels for 4%

profile of v3, /device:TPU:6, one launch (start us, length us, event | category | flops | bytes accessed | tf_op | source)
XLA Modules:
  0.0 142.7 jit_solution(655196679823621579)
XLA Ops:
  6.5 0.0 copy-start
  6.5 0.0 all-gather.4.cloned.1.call-start
  6.5 1.7 %pad_maximum_fusion = bf16[128,1024]{1,0:T(8,128)(2,1)} fusion(bf16[128,512]{1,0:T(8,128)(2,1)} %param.8, bf16[128,512]{1,0:T(8,128)(2,1)} %param.7), kind=kLoop, calls=%fused_computation.7 | loop fusion | flops 524288 | bytes 524288 | tf_op jit(solution)/shard_map/concatenate | solution.py:104
  8.3 0.0 all-gather.4.cloned.1.call-update
  9.0 0.0 copy-done
  9.0 6.9 %collective-permute-start = (bf16[128,256]{1,0:T(8,128)(2,1)S(1)}, bf16[128,256]{1,0:T(8,128)(2,1)S(1)}, u32[]{:S(2)}, u32[]{:S(2)}) collective-permute-start(bf16[128,256]{1,0:T(8,128)(2,1)S(1)} %constant_dynamic-slice_fusion), channel_id=1, source_target_pairs={{0,0},{1,1},{2,2},{3,3},{4,128},{5,129},{6,130},{7,131},{8,256},{9... | collective-permute-start | bytes 196616 | tf_op jit(solution)/shard_map/ppermute | solution.py:125
  15.9 6.4 %collective-permute-start.7 = (bf16[512,128]{1,0:T(8,128)(2,1)}, bf16[512,128]{1,0:T(8,128)(2,1)S(1)}, u32[]{:S(2)}, u32[]{:S(2)}) collective-permute-start(bf16[512,128]{1,0:T(8,128)(2,1)} %param.9), channel_id=1, source_target_pairs={{1,0},{257,1},{129,128},{385,129},{0,256},{256,257},{128,384},{384... | collective-permute-start | bytes 393224 | tf_op jit(solution)/shard_map/ppermute | solution.py:111
  22.3 1.6 %collective-permute-start.6 = (bf16[512,128]{1,0:T(8,128)(2,1)}, bf16[512,128]{1,0:T(8,128)(2,1)S(1)}, u32[]{:S(2)}, u32[]{:S(2)}) collective-permute-start(bf16[512,128]{1,0:T(8,128)(2,1)} %param.9), channel_id=1, source_target_pairs={{0,0},{256,1},{128,128},{384,129},{1,256},{257,257},{129,384},{385... | collective-permute-start | bytes 393224 | tf_op jit(solution)/shard_map/ppermute | solution.py:111
  23.9 0.0 collective-permute-done
  23.9 0.9 broadcast_in_dim.14
  24.7 8.1 %all-to-all-start = ((bf16[8,128,256]{2,1,0:T(8,128)(2,1)}), bf16[8,128,256]{2,1,0:T(8,128)(2,1)S(1)}, u32[]{:S(2)}, u32[]{:S(2)}) async-start(bf16[8,128,256]{2,1,0:T(8,128)(2,1)} %broadcast_in_dim.14), calls=%async_computation | async-start | bytes 1048576 | tf_op jit(solution)/shard_map/all_to_all | solution.py:128
  32.9 0.0 all-gather.6.cloned.1.call-start
  32.9 0.0 collective-permute-done.7
  32.9 0.0 collective-permute-done.6
  32.9 0.7 pad_maximum_fusion.1
  33.7 0.0 all-gather.6.cloned.1.call-update
  33.7 7.3 %all-to-all-done = bf16[8,128,256]{2,1,0:T(8,128)(2,1)S(1)} async-done(((bf16[8,128,256]{2,1,0:T(8,128)(2,1)}), bf16[8,128,256]{2,1,0:T(8,128)(2,1)S(1)}, u32[]{:S(2)}, u32[]{:S(2)}) %all-to-all-start) | async-done | bytes 524320 | tf_op jit(solution)/shard_map/all_to_all | solution.py:128
  41.0 0.0 copy-start.2
  41.0 1.9 %collective-permute-start.1 = (bf16[4,2,128,256]{3,2,1,0:T(8,128)(2,1)S(1)}, bf16[4,2,128,256]{3,2,1,0:T(8,128)(2,1)S(1)}, u32[]{:S(2)}, u32[]{:S(2)}) collective-permute-start(bf16[4,2,128,256]{3,2,1,0:T(8,128)(2,1)S(1)} %bitcast.26), channel_id=1, source_target_pairs={{0,1},{1,0},{2,3},{3,2},{4,5},{5,4},{6,7},{7,6},{8,9},{9,8},{10,11... | collective-permute-start | bytes 1572872 | tf_op jit(solution)/shard_map/ppermute | solution.py:130
  42.9 0.6 pad_add_fusion.where_ref
  43.6 0.0 copy-start.9
  43.6 0.0 copy-start.7
  43.6 1.2 collective-permute-done.1.theirs_ref
  44.8 0.0 copy-start.8
  44.8 12.7 %all-gather.4.cloned.1.call-done.w_ref = bf16[1024,1024]{1,0:T(8,128)(2,1)} async-done(((bf16[128,1024]{1,0:T(8,128)(2,1)}), bf16[1024,1024]{1,0:T(8,128)(2,1)}) %all-gather.4.cloned.1.call-update) | async-done | bytes 2097168 | tf_op jit(solution)/shard_map/all_gather | solution.py:104
  57.5 0.0 copy-done.2
  57.5 0.0 copy-done.8
  57.5 5.6 %first_product.1 = (bf16[4,128,1024]{2,1,0:T(8,128)(2,1)}, f32[128,1024]{1,0:T(8,128)}) custom-call(s32[2]{0:T(128)} %pad_add_fusion.where_ref, bf16[4,2,128,256]{3,2,1,0:T(8,128)(2,1)} %bitcast.27, bf16[4,2,128,256]{3,2,1,0:T(8,128)(2,1)} %copy-done.8, bf16[1024,1024]{1,0:T(8,128)(2,1)} %all-gather.4.cloned.1.call-done.w_ref), custom_call_target="tpu_custom_call" | custom-call | flops 1073741824 | bytes 5242880 | tf_op jit(solution)/shard_map/first_product/pallas_call | solution.py:35
  63.1 0.0 copy-start.1
  63.1 7.9 %all-to-all-start.1 = ((bf16[4,128,1024]{2,1,0:T(8,128)(2,1)}), bf16[4,128,1024]{2,1,0:T(8,128)(2,1)S(1)}, u32[]{:S(2)}, u32[]{:S(2)}) async-start(bf16[4,128,1024]{2,1,0:T(8,128)(2,1)} %get-tuple-element.12), calls=%async_computation.1 | async-start | bytes 2097152 | tf_op jit(solution)/shard_map/all_to_all | solution.py:133
  71.0 0.0 copy-done.9
  71.0 0.7 dynamic_slice.9
  72.4 0.0 copy-done.7
  72.4 0.1 multiply_convert_fusion.1
  72.5 4.8 %collective-permute-start.2 = (bf16[128]{0:T(256)(128)(2,1)S(1)}, bf16[128]{0:T(256)(128)(2,1)S(1)}, u32[]{:S(2)}, u32[]{:S(2)}) collective-permute-start(bf16[128]{0:T(256)(128)(2,1)S(1)} %multiply_convert_fusion.1), channel_id=1, source_target_pairs={{0,128},{128,0},{256,384},{384,256},{1,129},{129,1},{257,385},{385... | collective-permute-start | bytes 776 | tf_op jit(solution)/shard_map/ppermute | solution.py:142
  77.3 17.9 %all-to-all-done.1 = bf16[4,128,1024]{2,1,0:T(8,128)(2,1)S(1)} async-done(((bf16[4,128,1024]{2,1,0:T(8,128)(2,1)}), bf16[4,128,1024]{2,1,0:T(8,128)(2,1)S(1)}, u32[]{:S(2)}, u32[]{:S(2)}) %all-to-all-start.1) | async-done | bytes 1048608 | tf_op jit(solution)/shard_map/all_to_all | solution.py:133
  95.2 0.0 copy-done.1
  95.2 0.2 bitcast_add_fusion
  95.4 0.1 fusion.a_ref
  95.5 0.0 copy-start.3
  95.5 0.0 collective-permute-done.2
  95.5 3.2 %collective-permute-start.3 = (bf16[128,512]{1,0:T(8,128)(2,1)S(1)}, bf16[128,512]{1,0:T(8,128)(2,1)S(1)}, u32[]{:S(2)}, u32[]{:S(2)}) collective-permute-start(bf16[128,512]{1,0:T(8,128)(2,1)S(1)} %fusion.a_ref), channel_id=1, source_target_pairs={{0,128},{128,0},{256,384},{384,256},{1,129},{129,1},{257,385},{385... | collective-permute-start | bytes 393224 | tf_op jit(solution)/shard_map/ppermute | solution.py:146
  98.7 1.9 %collective-permute-start.4 = (bf16[128,512]{1,0:T(8,128)(2,1)S(1)}, bf16[128,512]{1,0:T(8,128)(2,1)S(1)}, u32[]{:S(2)}, u32[]{:S(2)}) collective-permute-start(bf16[128,512]{1,0:T(8,128)(2,1)S(1)} %fusion.a_ref), channel_id=1, source_target_pairs={{0,1},{1,0},{2,3},{3,2},{4,5},{5,4},{6,7},{7,6},{8,9},{9,8},{10,11... | collective-permute-start | bytes 393224 | tf_op jit(solution)/shard_map/ppermute | solution.py:148
  100.7 2.6 %collective-permute-done.3.b_ref = bf16[128,512]{1,0:T(8,128)(2,1)S(1)} collective-permute-done((bf16[128,512]{1,0:T(8,128)(2,1)S(1)}, bf16[128,512]{1,0:T(8,128)(2,1)S(1)}, u32[]{:S(2)}, u32[]{:S(2)}) %collective-permute-start.3) | collective-permute-done | bytes 131104 | tf_op jit(solution)/shard_map/ppermute | solution.py:146
  103.3 0.0 copy-start.4
  103.3 1.9 %collective-permute-start.5 = (bf16[128,512]{1,0:T(8,128)(2,1)S(1)}, bf16[128,512]{1,0:T(8,128)(2,1)S(1)}, u32[]{:S(2)}, u32[]{:S(2)}) collective-permute-start(bf16[128,512]{1,0:T(8,128)(2,1)S(1)} %collective-permute-done.3.b_ref), channel_id=1, source_target_pairs={{0,1},{1,0},{2,3},{3,2},{4,5},{5,4},{6,7},{7,6},{8,9},{9,8},{10,11... | collective-permute-start | bytes 393224 | tf_op jit(solution)/shard_map/ppermute | solution.py:148
  105.2 0.0 all-gather.6.cloned.1.call-done
  105.2 0.0 collective-permute-done.4.c_ref
  105.3 0.0 copy-start.5
  105.3 1.3 collective-permute-done.5.d_ref
  106.5 0.0 copy-start.6
  106.5 0.0 copy-done.3
  106.5 0.0 copy-done.4
  106.5 0.0 copy-done.5
  106.5 0.6 copy-done.6
  107.2 4.9 %second_product.1 = bf16[2,4,128,256]{3,2,1,0:T(8,128)(2,1)} custom-call(s32[2]{0:T(128)} %pad_add_fusion.where_ref, bf16[128,512]{1,0:T(8,128)(2,1)} %copy-done.3, bf16[128,512]{1,0:T(8,128)(2,1)} %copy-done.4, bf16[128,512]{1,0:T(8,128)(2,1)} %copy-done.5, bf16[128,512]{1,0:T(8,128)(2,1)} %copy-done.6, bf16[8,2,512,128]{3,2,1,0:T(8,128)(2,1)} %bitcast.24), custom_call_target="tpu_custom_call" | custom-call | flops 536870912 | bytes 4194304 | tf_op jit(solution)/shard_map/second_product/pallas_call | solution.py:78
  112.1 4.8 %all-to-all-start.2 = ((bf16[8,128,256]{2,1,0:T(8,128)(2,1)}), bf16[8,128,256]{2,1,0:T(8,128)(2,1)S(1)}, u32[]{:S(2)}, u32[]{:S(2)}) async-start(bf16[8,128,256]{2,1,0:T(8,128)(2,1)} %bitcast.25), calls=%async_computation.2 | async-start | bytes 1048576 | tf_op jit(solution)/shard_map/all_to_all | solution.py:150
  116.9 7.8 %all-to-all-done.2 = bf16[8,128,256]{2,1,0:T(8,128)(2,1)S(1)} async-done(((bf16[8,128,256]{2,1,0:T(8,128)(2,1)}), bf16[8,128,256]{2,1,0:T(8,128)(2,1)S(1)}, u32[]{:S(2)}, u32[]{:S(2)}) %all-to-all-start.2) | async-done | bytes 524320 | tf_op jit(solution)/shard_map/all_to_all | solution.py:150
  124.7 0.1 convert_reduce_fusion
  124.7 0.1 multiply_convert_fusion
  124.8 2.4 %collective-permute-start.8 = (bf16[128,256]{1,0:T(8,128)(2,1)S(1)}, bf16[128,256]{1,0:T(8,128)(2,1)S(1)}, u32[]{:S(2)}, u32[]{:S(2)}) collective-permute-start(bf16[128,256]{1,0:T(8,128)(2,1)S(1)} %multiply_convert_fusion), channel_id=1, source_target_pairs={{0,0},{1,136},{2,2},{3,138},{4,1},{5,137},{6,3},{7,139},{8,128},{9... | collective-permute-start | bytes 196616 | tf_op jit(solution)/shard_map/ppermute | solution.py:162
  127.2 7.9 %collective-permute-done.8 = bf16[128,256]{1,0:T(8,128)(2,1)S(1)} collective-permute-done((bf16[128,256]{1,0:T(8,128)(2,1)S(1)}, bf16[128,256]{1,0:T(8,128)(2,1)S(1)}, u32[]{:S(2)}, u32[]{:S(2)}) %collective-permute-start.8) | collective-permute-done | bytes 65568 | tf_op jit(solution)/shard_map/ppermute | solution.py:162
  135.2 0.7 pad_maximum_fusion.2
  (3 shorter events, 0.0 us)
Async XLA Ops:
  6.5 2.4 %copy-start = (bf16[256,256]{1,0:T(8,128)(2,1)S(1)}, bf16[256,256]{1,0:T(8,128)(2,1)}, u32[]{:S(2)}) copy-start(bf16[256,256]{1,0:T(8,128)(2,1)} %param.6) | copy-start | bytes 393220
  6.5 50.9 %all-gather.4.cloned.1.call-start = ((), (), s32[]{:S(2)}) async-start(), calls=%async_computation.3 | async-start | bytes 2359296 | tf_op jit(solution)/shard_map/all_gather | solution.py:104
  9.0 14.9 %collective-permute-start = (bf16[128,256]{1,0:T(8,128)(2,1)S(1)}, bf16[128,256]{1,0:T(8,128)(2,1)S(1)}, u32[]{:S(2)}, u32[]{:S(2)}) collective-permute-start(bf16[128,256]{1,0:T(8,128)(2,1)S(1)} %constant_dynamic-slice_fusion), channel_id=1, source_target_pairs={{0,0},{1,1},{2,2},{3,3},{4,128},{5,129},{6,130},{7,131},{8,256},{9... | collective-permute-start | bytes 196616 | tf_op jit(solution)/shard_map/ppermute | solution.py:125
  15.9 17.0 %collective-permute-start.7 = (bf16[512,128]{1,0:T(8,128)(2,1)}, bf16[512,128]{1,0:T(8,128)(2,1)S(1)}, u32[]{:S(2)}, u32[]{:S(2)}) collective-permute-start(bf16[512,128]{1,0:T(8,128)(2,1)} %param.9), channel_id=1, source_target_pairs={{1,0},{257,1},{129,128},{385,129},{0,256},{256,257},{128,384},{384... | collective-permute-start | bytes 393224 | tf_op jit(solution)/shard_map/ppermute | solution.py:111
  22.3 10.6 %collective-permute-start.6 = (bf16[512,128]{1,0:T(8,128)(2,1)}, bf16[512,128]{1,0:T(8,128)(2,1)S(1)}, u32[]{:S(2)}, u32[]{:S(2)}) collective-permute-start(bf16[512,128]{1,0:T(8,128)(2,1)} %param.9), channel_id=1, source_target_pairs={{0,0},{256,1},{128,128},{384,129},{1,256},{257,257},{129,384},{385... | collective-permute-start | bytes 393224 | tf_op jit(solution)/shard_map/ppermute | solution.py:111
  24.7 16.3 %all-to-all-start = ((bf16[8,128,256]{2,1,0:T(8,128)(2,1)}), bf16[8,128,256]{2,1,0:T(8,128)(2,1)S(1)}, u32[]{:S(2)}, u32[]{:S(2)}) async-start(bf16[8,128,256]{2,1,0:T(8,128)(2,1)} %broadcast_in_dim.14), calls=%async_computation | async-start | bytes 1048576 | tf_op jit(solution)/shard_map/all_to_all | solution.py:128
  32.9 72.3 %all-gather.6.cloned.1.call-start = ((), (), s32[]{:S(2)}) async-start(), calls=%async_computation.4 | async-start | bytes 2359296 | tf_op jit(solution)/shard_map/all_gather | solution.py:112
  41.0 16.5 %copy-start.2 = (bf16[8,128,256]{2,1,0:T(8,128)(2,1)}, bf16[8,128,256]{2,1,0:T(8,128)(2,1)S(1)}, u32[]{:S(2)}) copy-start(bf16[8,128,256]{2,1,0:T(8,128)(2,1)S(1)} %all-to-all-done) | copy-start | bytes 1572868
  41.0 3.8 %collective-permute-start.1 = (bf16[4,2,128,256]{3,2,1,0:T(8,128)(2,1)S(1)}, bf16[4,2,128,256]{3,2,1,0:T(8,128)(2,1)S(1)}, u32[]{:S(2)}, u32[]{:S(2)}) collective-permute-start(bf16[4,2,128,256]{3,2,1,0:T(8,128)(2,1)S(1)} %bitcast.26), channel_id=1, source_target_pairs={{0,1},{1,0},{2,3},{3,2},{4,5},{5,4},{6,7},{7,6},{8,9},{9,8},{10,11... | collective-permute-start | bytes 1572872 | tf_op jit(solution)/shard_map/ppermute | solution.py:130
  43.6 27.4 %copy-start.9 = (s32[2]{0:T(128)S(1)}, s32[2]{0:T(128)}, u32[]{:S(2)}) copy-start(s32[2]{0:T(128)} %param.10) | copy-start | bytes 28
  43.6 28.8 %copy-start.7 = (s32[256]{0:T(256)S(1)}, s32[256]{0:T(256)}, u32[]{:S(2)}) copy-start(s32[256]{0:T(256)} %param.11) | copy-start | bytes 3076
  44.8 12.7 %copy-start.8 = (bf16[4,2,128,256]{3,2,1,0:T(8,128)(2,1)}, bf16[4,2,128,256]{3,2,1,0:T(8,128)(2,1)S(1)}, u32[]{:S(2)}) copy-start(bf16[4,2,128,256]{3,2,1,0:T(8,128)(2,1)S(1)} %collective-permute-done.1.theirs_ref) | copy-start | bytes 1572868
  63.1 32.1 %copy-start.1 = (f32[128,1024]{1,0:T(8,128)S(1)}, f32[128,1024]{1,0:T(8,128)}, u32[]{:S(2)}) copy-start(f32[128,1024]{1,0:T(8,128)} %get-tuple-element.11) | copy-start | bytes 1572868
  63.1 32.1 %all-to-all-start.1 = ((bf16[4,128,1024]{2,1,0:T(8,128)(2,1)}), bf16[4,128,1024]{2,1,0:T(8,128)(2,1)S(1)}, u32[]{:S(2)}, u32[]{:S(2)}) async-start(bf16[4,128,1024]{2,1,0:T(8,128)(2,1)} %get-tuple-element.12), calls=%async_computation.1 | async-start | bytes 2097152 | tf_op jit(solution)/shard_map/all_to_all | solution.py:133
  72.5 23.1 %collective-permute-start.2 = (bf16[128]{0:T(256)(128)(2,1)S(1)}, bf16[128]{0:T(256)(128)(2,1)S(1)}, u32[]{:S(2)}, u32[]{:S(2)}) collective-permute-start(bf16[128]{0:T(256)(128)(2,1)S(1)} %multiply_convert_fusion.1), channel_id=1, source_target_pairs={{0,128},{128,0},{256,384},{384,256},{1,129},{129,1},{257,385},{385... | collective-permute-start | bytes 776 | tf_op jit(solution)/shard_map/ppermute | solution.py:142
  95.5 11.0 %copy-start.3 = (bf16[128,512]{1,0:T(8,128)(2,1)}, bf16[128,512]{1,0:T(8,128)(2,1)S(1)}, u32[]{:S(2)}) copy-start(bf16[128,512]{1,0:T(8,128)(2,1)S(1)} %fusion.a_ref) | copy-start | bytes 393220
  95.5 7.8 %collective-permute-start.3 = (bf16[128,512]{1,0:T(8,128)(2,1)S(1)}, bf16[128,512]{1,0:T(8,128)(2,1)S(1)}, u32[]{:S(2)}, u32[]{:S(2)}) collective-permute-start(bf16[128,512]{1,0:T(8,128)(2,1)S(1)} %fusion.a_ref), channel_id=1, source_target_pairs={{0,128},{128,0},{256,384},{384,256},{1,129},{129,1},{257,385},{385... | collective-permute-start | bytes 393224 | tf_op jit(solution)/shard_map/ppermute | solution.py:146
  98.7 6.5 %collective-permute-start.4 = (bf16[128,512]{1,0:T(8,128)(2,1)S(1)}, bf16[128,512]{1,0:T(8,128)(2,1)S(1)}, u32[]{:S(2)}, u32[]{:S(2)}) collective-permute-start(bf16[128,512]{1,0:T(8,128)(2,1)S(1)} %fusion.a_ref), channel_id=1, source_target_pairs={{0,1},{1,0},{2,3},{3,2},{4,5},{5,4},{6,7},{7,6},{8,9},{9,8},{10,11... | collective-permute-start | bytes 393224 | tf_op jit(solution)/shard_map/ppermute | solution.py:148
  103.3 3.2 %copy-start.4 = (bf16[128,512]{1,0:T(8,128)(2,1)}, bf16[128,512]{1,0:T(8,128)(2,1)S(1)}, u32[]{:S(2)}) copy-start(bf16[128,512]{1,0:T(8,128)(2,1)S(1)} %collective-permute-done.3.b_ref) | copy-start | bytes 393220
  103.3 3.2 %collective-permute-start.5 = (bf16[128,512]{1,0:T(8,128)(2,1)S(1)}, bf16[128,512]{1,0:T(8,128)(2,1)S(1)}, u32[]{:S(2)}, u32[]{:S(2)}) collective-permute-start(bf16[128,512]{1,0:T(8,128)(2,1)S(1)} %collective-permute-done.3.b_ref), channel_id=1, source_target_pairs={{0,1},{1,0},{2,3},{3,2},{4,5},{5,4},{6,7},{7,6},{8,9},{9,8},{10,11... | collective-permute-start | bytes 393224 | tf_op jit(solution)/shard_map/ppermute | solution.py:148
  105.3 1.3 copy-start.5
  106.5 0.7 copy-start.6
  112.1 12.6 %all-to-all-start.2 = ((bf16[8,128,256]{2,1,0:T(8,128)(2,1)}), bf16[8,128,256]{2,1,0:T(8,128)(2,1)S(1)}, u32[]{:S(2)}, u32[]{:S(2)}) async-start(bf16[8,128,256]{2,1,0:T(8,128)(2,1)} %bitcast.25), calls=%async_computation.2 | async-start | bytes 1048576 | tf_op jit(solution)/shard_map/all_to_all | solution.py:150
  124.8 10.4 %collective-permute-start.8 = (bf16[128,256]{1,0:T(8,128)(2,1)S(1)}, bf16[128,256]{1,0:T(8,128)(2,1)S(1)}, u32[]{:S(2)}, u32[]{:S(2)}) collective-permute-start(bf16[128,256]{1,0:T(8,128)(2,1)S(1)} %multiply_convert_fusion), channel_id=1, source_target_pairs={{0,0},{1,136},{2,2},{3,138},{4,1},{5,137},{6,3},{7,139},{8,128},{9... | collective-permute-start | bytes 196616 | tf_op jit(solution)/shard_map/ppermute | solution.py:162
Sparse Core Ops, SparseCore 0:
  9.4 47.9 all-gather.3
  59.5 43.0 all-gather.5

commit v4 on v2

--- a/solution.py
+++ b/solution.py
@@ -78,40 +78,49 @@
     )(where, mine, theirs, weights)
 
 
-def second_product(where, hidden, near, far):
-    rows, hidden_count = hidden.shape
+def second_product(where, mine, theirs, near, passed, far):
+    rows, depth = mine.shape
     ranks, others = far.shape[:2]
     groups = others + 1
-    panels = hidden_count // LANES
+    panels = depth // LANES
+    quads = ranks // 2
 
-    def body(where_ref, hidden_ref, near_ref, far_ref, out_ref):
-        value = hidden_ref[...]
+    def body(where_ref, mine_ref, theirs_ref, near_ref, passed_ref, far_ref, out_ref):
+        core = where_ref[1]
+        left, right = mine_ref[...], theirs_ref[...]
         for s in range(groups):
-            if s == 0:
-                halves = [near_ref[i].reshape(hidden_count, LANES) for i in range(2)]
-            else:
-                halves = [far_ref[i, s - 1] for i in range(2)]
-            part = jnp.dot(value, jnp.concatenate(halves, 1), preferred_element_type=F32)
+            own, other = [], []
+            for low in range(2):
+                if s == 0:
+                    own.append(near_ref[core * 2 + low].reshape(depth, LANES))
+                    other.append(passed_ref[0, low].reshape(depth, LANES))
+                else:
+                    own.append(far_ref[core * 2 + low, s - 1])
+                    other.append(far_ref[(1 - core) * 2 + low, s - 1])
+            part = jnp.dot(left, jnp.concatenate(own, 1), preferred_element_type=F32)
+            part = part + jnp.dot(right, jnp.concatenate(other, 1), preferred_element_type=F32)
             out_ref[lax.rem(where_ref[0] + s, groups), 0] = part.astype(BF16)
 
     return pl.pallas_call(
         body,
         grid_spec=pltpu.PrefetchScalarGridSpec(
             num_scalar_prefetch=1,
-            grid=(ranks // 2,),
+            grid=(2,),
             in_specs=[
-                pl.BlockSpec(hidden.shape, lambda j, s: (0, 0)),
-                pl.BlockSpec((2, panels) + near.shape[2:], lambda j, s: (j, 2, 0, 0)),
-                pl.BlockSpec((2,) + far.shape[1:], lambda j, s: (j, 0, 0, 0)),
+                pl.BlockSpec(mine.shape, lambda j, s: (0, 0)),
+                pl.BlockSpec(mine.shape, lambda j, s: (0, 0)),
+                pl.BlockSpec((quads, panels) + near.shape[2:], lambda j, s: (j, 2, 0, 0)),
+                pl.BlockSpec((1,) + passed.shape[1:], lambda j, s: (j, 0, 0, 0, 0)),
+                pl.BlockSpec((quads,) + far.shape[1:], lambda j, s: (j, 0, 0, 0)),
             ],
             out_specs=pl.BlockSpec((groups, 1, rows, 2 * LANES), lambda j, s: (0, j, 0, 0)),
         ),
-        out_shape=jax.ShapeDtypeStruct((groups, ranks // 2, rows, 2 * LANES), BF16),
+        out_shape=jax.ShapeDtypeStruct((groups, 2, rows, 2 * LANES), BF16),
         cost_estimate=pl.CostEstimate(
-            flops=2 * rows * hidden_count * groups * ranks * LANES, bytes_accessed=5 << 20, transcendentals=0
+            flops=2 * rows * 2 * depth * groups * 4 * LANES, bytes_accessed=5 << 20, transcendentals=0
         ),
         name="second_product",
-    )(where, hidden, near, far)
+    )(where, mine, theirs, near, passed, far)
 
 
 def per_device(tokens, w_gate, w_up, w_down, pattern, gate_code):
@@ -124,9 +133,18 @@
     where = jnp.stack([zh, lax.axis_index("c")]).astype(jnp.int32)
 
     near = lax.all_gather(pack(w_gate, w_up, w_down), "y", axis=0, tiled=False)
-    columns = lax.all_gather(w_down, "zh", axis=0, tiled=False)
-    others = jnp.stack([lax.dynamic_index_in_dim(columns, (zh + s) % groups, keepdims=False) for s in range(1, groups)])
-    far = lax.all_gather(others, "y", axis=0, tiled=False)
+    core = lax.axis_index("c")
+    blocks = []
+    for shift in range(1, groups):
+        moves = []
+        for z in range(groups):
+            for y in range(ranks):
+                for c in range(2):
+                    bit = y // 2 % 2
+                    target = ((z - shift) % groups * ranks + y + 2 * (c - bit)) * 2 + bit
+                    moves.append(((z * ranks + y) * 2 + c, target))
+        blocks.append(lax.ppermute(w_down, ("zh", "y", "c"), moves))
+    far = lax.all_gather(jnp.stack(blocks), "y", axis=0, tiled=False)
 
     chosen = jnp.where(pattern[0] > 0, 0, 1)
     rows = lax.dynamic_slice_in_dim(tokens, chosen * block_rows, block_rows, 0)
@@ -146,6 +164,11 @@
     theirs = lax.ppermute(mine, "c", [(0, 1), (1, 0)])
 
     sent, own = first_product(where, mine, theirs, near)
+    cores = [(0, 1), (1, 0)]
+    later, sent = lax.optimization_barrier((near, sent))
+    later = later.reshape((2, 2, 2) + near.shape[1:])
+    later = lax.dynamic_index_in_dim(later, 1 - core, 1, keepdims=False)[:, :, -(near.shape[1] // 3) :]
+    passed = lax.ppermute(later, "c", cores)
     got = lax.all_to_all(sent, "zh", split_axis=0, concat_axis=0, tiled=True)
     total = own
     for k in range(groups):
@@ -153,8 +176,9 @@
     gate, up = jnp.split(total, 2, 1)
     hidden = (jax.nn.silu(gate) * up).astype(BF16)
 
-    part = second_product(where, hidden, near, far)
-    parts = lax.all_to_all(part.reshape(size, block_rows, width), EXP, split_axis=0, concat_axis=0, tiled=True)
+    hidden, passed = lax.optimization_barrier((hidden, passed))
+    part = second_product(where, hidden, lax.ppermute(hidden, "c", cores), near, passed, far)
+    parts = lax.all_to_all(part.reshape(chips, block_rows, width), ("zl", "x"), split_axis=0, concat_axis=0, tiled=True)
     summed = jnp.sum(parts.astype(F32), 0)
     result = row_scale.reshape(block_count, block_rows, 1) * summed[None]
     return result.astype(BF16).reshape(row_count, width)

time: 147 us -> 139 us (0.946)
  starting transfers between devices: 21.3 us -> 39.7 us
  blocking collectives: 35.2 us -> 19.3 us
  waiting for transfers between devices: 56.5 us -> 45.9 us
  local copies, waits for them, and re-layouts: 0.09 us -> 1.76 us
    all_gather x1 -> x0, blocking collectives: 21.9 us -> none  [per_device(): columns = lax.all_gather(w_down, 'zh', axis=0, tiled=False)]
    ppermute x0 -> x5, starting transfers between devices: none -> 21.6 us  [the longest x3 17.7 us: per_device(): blocks.append(lax.ppermute(w_down, ('zh', 'y', 'c'), moves))]
    all_to_all x1, waiting for transfers between devices: 14.8 us -> 6.78 us  [per_device(): lax.all_to_all(part.reshape(chips, block_rows, width), ('zl', 'x'), split...]
    all_to_all x1, waiting for transfers between devices: 25 us -> 18.9 us  [per_device(): got = lax.all_to_all(sent, 'zh', split_axis=0, concat_axis=0, tiled=True)]
    all_to_all x1, blocking collectives: 13.3 us -> 19.3 us  [per_device(): lax.all_to_all(copies, ('zl', 'x'), split_axis=0, concat_axis=0, tiled=True)]
    ppermute x0 -> x5, waiting for transfers between devices: none -> 5.82 us  [the longest x3 5.81 us: per_device(): blocks.append(lax.ppermute(w_down, ('zh', 'y', 'c'), moves))]
    all_to_all x1, starting transfers between devices: 7.38 us -> 4.24 us  [per_device(): got = lax.all_to_all(sent, 'zh', split_axis=0, concat_axis=0, tiled=True)]
    all_gather x1, waiting for transfers between devices: 2.79 us -> 0.01 us  [per_device(): near = lax.all_gather(pack(w_gate, w_up, w_down), 'y', axis=0, tiled=False)]
  transfers between devices with their start and end apart: 6 -> 11, of which waited for: 6 -> 7; matrix products, arithmetic and copies ran while one was open for 3% -> 3% of each run, Pallas kernels for 4% -> 4%
where the time goes in v4:
time: 139 us; the launch traced here: 137 us
  waiting for transfers between devices  45.9 us (33%)
  starting transfers between devices  39.7 us (29%)
  blocking collectives  19.3 us (14%)
  between operations  14.2 us (10%)
  Pallas kernels  12.2 us (9%)
  other arithmetic  4.04 us (3%)
  local copies, waits for them, and re-layouts  1.76 us (1%)
    all_to_all x1, blocking collectives, per_device(): lax.all_to_all(copies, ('zl', 'x'), split_axis=0, concat_axis=0, tiled=True)  19.3 us
    all_to_all x1, waiting for transfers between devices, per_device(): got = lax.all_to_all(sent, 'zh', split_axis=0, concat_axis=0, tiled=True)  18.9 us
    ppermute x3, starting transfers between devices, per_device(): blocks.append(lax.ppermute(w_down, ('zh', 'y', 'c'), moves))  17.7 us
    all_gather x1, waiting for transfers between devices, per_device(): far = lax.all_gather(jnp.stack(blocks), 'y', axis=0, tiled=False)  9.73 us
    all_to_all x1, waiting for transfers between devices, per_device(): lax.all_to_all(part.reshape(chips, block_rows, width), ('zl', 'x'), split...  6.78 us
    ppermute x1, starting transfers between devices, per_device(): rows = lax.ppermute(rows, ('zh',) + EXP, swap)  6.02 us
    all_to_all x1, starting transfers between devices, per_device(): lax.all_to_all(part.reshape(chips, block_rows, width), ('zl', 'x'), split...  5.87 us
    pallas_call x1, Pallas kernels, first_product(): pl.pallas_call(body, grid_spec=pltpu.PrefetchScalarGridSpec(num_scalar_pr...  5.84 us
  transfers between devices with their start and end apart: 11, of which 7 were waited for; matrix products, arithmetic and copies ran while one was open for 3% of the time, Pallas kernels for 4%

profile of v4, /device:TPU:6, one launch (start us, length us, event | category | flops | bytes accessed | tf_op | source)
XLA Modules:
  0.0 137.1 jit_solution(15324494779924944778)
XLA Ops:
  6.5 0.0 copy-start
  6.5 0.0 all-gather.5.cloned.1.call-start
  6.5 1.9 %pack.1 = bf16[12,128,128]{2,1,0:T(8,128)(2,1)} custom-call(bf16[128,512]{1,0:T(8,128)(2,1)} %gate_ref.1, bf16[128,512]{1,0:T(8,128)(2,1)} %up_ref.1, bf16[512,128]{1,0:T(8,128)(2,1)} %down_ref.1), custom_call_target="tpu_custom_call" | custom-call | tf_op jit(solution)/shard_map/pack/pallas_call | solution.py:25
  8.4 0.0 all-gather.5.cloned.1.call-update
  8.5 0.0 all-gather.7.cloned.1.call-start
  8.5 10.9 %collective-permute-start.4 = (bf16[512,128]{1,0:T(8,128)(2,1)}, bf16[512,128]{1,0:T(8,128)(2,1)S(1)}, u32[]{:S(2)}, u32[]{:S(2)}) collective-permute-start(bf16[512,128]{1,0:T(8,128)(2,1)} %down_ref.1), channel_id=1, source_target_pairs={{0,384},{1,416},{16,400},{17,432},{32,385},{33,417},{48,401},{49,4... | collective-permute-start | bytes 393224 | tf_op jit(solution)/shard_map/ppermute | solution.py:146
  19.5 1.9 %collective-permute-start.5 = (bf16[512,128]{1,0:T(8,128)(2,1)}, bf16[512,128]{1,0:T(8,128)(2,1)S(1)}, u32[]{:S(2)}, u32[]{:S(2)}) collective-permute-start(bf16[512,128]{1,0:T(8,128)(2,1)} %down_ref.1), channel_id=1, source_target_pairs={{0,256},{1,288},{16,272},{17,304},{32,257},{33,289},{48,273},{49,3... | collective-permute-start | bytes 393224 | tf_op jit(solution)/shard_map/ppermute | solution.py:146
  21.4 4.8 %collective-permute-start.6 = (bf16[512,128]{1,0:T(8,128)(2,1)}, bf16[512,128]{1,0:T(8,128)(2,1)S(1)}, u32[]{:S(2)}, u32[]{:S(2)}) collective-permute-start(bf16[512,128]{1,0:T(8,128)(2,1)} %down_ref.1), channel_id=1, source_target_pairs={{0,128},{1,160},{16,144},{17,176},{32,129},{33,161},{48,145},{49,1... | collective-permute-start | bytes 393224 | tf_op jit(solution)/shard_map/ppermute | solution.py:146
  26.2 5.6 %collective-permute-done.4 = bf16[512,128]{1,0:T(8,128)(2,1)S(1)} collective-permute-done((bf16[512,128]{1,0:T(8,128)(2,1)}, bf16[512,128]{1,0:T(8,128)(2,1)S(1)}, u32[]{:S(2)}, u32[]{:S(2)}) %collective-permute-start.4) | collective-permute-done | bytes 131104 | tf_op jit(solution)/shard_map/ppermute | solution.py:146
  31.8 0.0 collective-permute-done.5
  31.8 0.2 collective-permute-done.6
  32.0 0.8 pad_maximum_fusion
  32.8 0.0 all-gather.7.cloned.1.call-update
  33.5 0.0 copy-done
  33.5 6.0 %collective-permute-start = (bf16[128,256]{1,0:T(8,128)(2,1)S(1)}, bf16[128,256]{1,0:T(8,128)(2,1)S(1)}, u32[]{:S(2)}, u32[]{:S(2)}) collective-permute-start(bf16[128,256]{1,0:T(8,128)(2,1)S(1)} %constant_dynamic-slice_fusion), channel_id=1, source_target_pairs={{0,0},{1,1},{2,2},{3,3},{4,128},{5,129},{6,130},{7,131},{8,256},{9... | collective-permute-start | bytes 196616 | tf_op jit(solution)/shard_map/ppermute | solution.py:159
  39.6 3.4 %collective-permute-done = bf16[128,256]{1,0:T(8,128)(2,1)S(1)} collective-permute-done((bf16[128,256]{1,0:T(8,128)(2,1)S(1)}, bf16[128,256]{1,0:T(8,128)(2,1)S(1)}, u32[]{:S(2)}, u32[]{:S(2)}) %collective-permute-start) | collective-permute-done | bytes 65568 | tf_op jit(solution)/shard_map/ppermute | solution.py:159
  43.0 19.3 %all_to_all.15 = bf16[8,128,256]{2,1,0:T(8,128)(2,1)S(1)} all-to-all(bf16[8,128,256]{2,1,0:T(8,128)(2,1)S(1)} %broadcast_in_dim.18), channel_id=1, replica_groups=mesh['zh'=4,'y'=8,'zl'=2,'x'=4,'c'=2] {'zl','x'}, dimensions={0} | all-to-all | bytes 1048576 | tf_op jit(solution)/shard_map/all_to_all | solution.py:162
  62.3 0.0 copy-start.2
  62.3 1.9 %collective-permute-start.1 = (bf16[4,2,128,256]{3,2,1,0:T(8,128)(2,1)S(1)}, bf16[4,2,128,256]{3,2,1,0:T(8,128)(2,1)S(1)}, u32[]{:S(2)}, u32[]{:S(2)}) collective-permute-start(bf16[4,2,128,256]{3,2,1,0:T(8,128)(2,1)S(1)} %bitcast.44), channel_id=1, source_target_pairs={{0,1},{1,0},{2,3},{3,2},{4,5},{5,4},{6,7},{7,6},{8,9},{9,8},{10,11... | collective-permute-start | bytes 1572872 | tf_op jit(solution)/shard_map/ppermute | solution.py:164
  64.2 0.6 pad_add_fusion.where_ref
  64.9 1.2 collective-permute-done.1.theirs_ref
  66.1 0.0 copy-start.4
  66.1 0.0 all-gather.5.cloned.1.call-done
  66.1 0.0 copy-done.2
  66.1 0.8 copy-done.4
  66.9 0.0 copy-start.1
  66.9 5.8 %first_product.1 = (bf16[4,128,1024]{2,1,0:T(8,128)(2,1)}, f32[128,1024]{1,0:T(8,128)}) custom-call(s32[2]{0:T(128)} %pad_add_fusion.where_ref, bf16[4,2,128,256]{3,2,1,0:T(8,128)(2,1)} %bitcast.45, bf16[4,2,128,256]{3,2,1,0:T(8,128)(2,1)} %copy-done.4, bf16[8,12,128,128]{3,2,1,0:T(8,128)(2,1)} %bitcast.40), custom_call_target="tpu_custom_call" | custom-call | flops 1073741824 | bytes 5242880 | tf_op jit(solution)/shard_map/first_product/pallas_call | solution.py:55
  72.8 4.2 %all-to-all-start.1 = ((bf16[4,128,1024]{2,1,0:T(8,128)(2,1)}), bf16[4,128,1024]{2,1,0:T(8,128)(2,1)}, u32[]{:S(2)}, u32[]{:S(2)}) async-start(bf16[4,128,1024]{2,1,0:T(8,128)(2,1)} %get-tuple-element.13), calls=%async_computation.1 | async-start | bytes 2097152 | tf_op jit(solution)/shard_map/all_to_all | solution.py:172
  77.0 0.0 copy-done.1
  77.0 0.2 dynamic-slice_bitcast_fusion
  77.3 2.0 %collective-permute-start.2 = (bf16[2,2,4,128,128]{4,3,2,1,0:T(8,128)(2,1)S(1)}, bf16[2,2,4,128,128]{4,3,2,1,0:T(8,128)(2,1)S(1)}, u32[]{:S(2)}, u32[]{:S(2)}) collective-permute-start(bf16[2,2,4,128,128]{4,3,2,1,0:T(8,128)(2,1)S(1)} %slice.28), channel_id=1, source_target_pairs={{0,1},{1,0},{2,3},{3,2},{4,5},{5,4},{6,7},{7,6},{8,9},{9,8},{10,11... | collective-permute-start | bytes 1572872 | tf_op jit(solution)/shard_map/ppermute | solution.py:171
  79.3 18.9 %all-to-all-done.1 = bf16[4,128,1024]{2,1,0:T(8,128)(2,1)} async-done(((bf16[4,128,1024]{2,1,0:T(8,128)(2,1)}), bf16[4,128,1024]{2,1,0:T(8,128)(2,1)}, u32[]{:S(2)}, u32[]{:S(2)}) %all-to-all-start.1) | async-done | bytes 1048608 | tf_op jit(solution)/shard_map/all_to_all | solution.py:172
  98.3 1.6 %bitcast_add_fusion = f32[128,1024]{1,0:T(8,128)S(1)} fusion(f32[128,1024]{1,0:T(8,128)} %get-tuple-element.11, bf16[4,128,1024]{2,1,0:T(8,128)(2,1)} %all-to-all-done.1, pred[]{:T(512)S(6)} %eq.15, pred[]{:T(512)S(6)} %eq.14, pred[]{:T(512)S(6)} %eq.13, pred[]{:T(512)S(6)} %eq.12), kind=kLoop, calls=%fused_computation.2 | loop fusion | flops 1572864 | bytes 2097156 | tf_op jit(solution)/shard_map/add | solution.py:175
  99.8 0.1 fusion.mine_ref
  99.9 0.0 copy-start.3
  99.9 0.0 collective-permute-done.2.passed_ref
  100.0 0.0 copy-start.5
  100.0 1.9 %collective-permute-start.3 = (bf16[128,512]{1,0:T(8,128)(2,1)S(1)}, bf16[128,512]{1,0:T(8,128)(2,1)S(1)}, u32[]{:S(2)}, u32[]{:S(2)}) collective-permute-start(bf16[128,512]{1,0:T(8,128)(2,1)S(1)} %fusion.mine_ref), channel_id=1, source_target_pairs={{0,1},{1,0},{2,3},{3,2},{4,5},{5,4},{6,7},{7,6},{8,9},{9,8},{10,11... | collective-permute-start | bytes 393224 | tf_op jit(solution)/shard_map/ppermute | solution.py:180
  101.9 9.7 %all-gather.7.cloned.1.call-done = bf16[24,512,128]{2,1,0:T(8,128)(2,1)} async-done(((bf16[3,512,128]{2,1,0:T(8,128)(2,1)}), bf16[24,512,128]{2,1,0:T(8,128)(2,1)}) %all-gather.7.cloned.1.call-update) | async-done | bytes 3145744 | tf_op jit(solution)/shard_map/all_gather | solution.py:147
  111.6 0.0 collective-permute-done.3.theirs_ref
  111.6 0.0 copy-start.6
  111.6 0.0 copy-done.3
  111.6 0.0 copy-done.5
  111.6 0.6 copy-done.6
  112.3 0.0 copy-start.8
  112.3 0.0 copy-start.7
  112.3 4.5 %second_product.1 = bf16[4,2,128,256]{3,2,1,0:T(8,128)(2,1)} custom-call(s32[2]{0:T(128)} %pad_add_fusion.where_ref, bf16[128,512]{1,0:T(8,128)(2,1)} %copy-done.3, bf16[128,512]{1,0:T(8,128)(2,1)} %copy-done.6, bf16[8,12,128,128]{3,2,1,0:T(8,128)(2,1)} %bitcast.41, bf16[2,2,4,128,128]{4,3,2,1,0:T(8,128)(2,1)} %copy-done.5, bf16[8,3,512,128]{3,2,1,0:T(8,128)(2,1)} %bitcast.43), custom_call_target="tpu_custom_call" | custom-call | flops 536870912 | bytes 5242880 | tf_op jit(solution)/shard_map/second_product/pallas_call | solution.py:104
  116.7 5.9 %all-to-all-start.2 = ((bf16[8,128,256]{2,1,0:T(8,128)(2,1)}), bf16[8,128,256]{2,1,0:T(8,128)(2,1)S(1)}, u32[]{:S(2)}, u32[]{:S(2)}) async-start(bf16[8,128,256]{2,1,0:T(8,128)(2,1)} %bitcast.46), calls=%async_computation.2 | async-start | bytes 1048576 | tf_op jit(solution)/shard_map/all_to_all | solution.py:181
  122.6 0.0 copy-done.8
  122.6 0.0 copy-done.7
  122.6 0.1 fusion.3
  122.7 6.8 %all-to-all-done.2 = bf16[8,128,256]{2,1,0:T(8,128)(2,1)S(1)} async-done(((bf16[8,128,256]{2,1,0:T(8,128)(2,1)}), bf16[8,128,256]{2,1,0:T(8,128)(2,1)S(1)}, u32[]{:S(2)}, u32[]{:S(2)}) %all-to-all-start.2) | async-done | bytes 524320 | tf_op jit(solution)/shard_map/all_to_all | solution.py:181
  129.5 0.1 convert_reduce_fusion
  129.5 0.8 fusion.1
  (4 shorter events, 0.1 us)
Async XLA Ops:
  6.5 27.0 %copy-start = (bf16[256,256]{1,0:T(8,128)(2,1)S(1)}, bf16[256,256]{1,0:T(8,128)(2,1)}, u32[]{:S(2)}) copy-start(bf16[256,256]{1,0:T(8,128)(2,1)} %param.6) | copy-start | bytes 393220
  6.5 59.6 %all-gather.5.cloned.1.call-start = ((), (), s32[]{:S(2)}) async-start(), calls=%async_computation.3 | async-start | bytes 3538944 | tf_op jit(solution)/shard_map/all_gather | solution.py:135
  8.5 103.2 %all-gather.7.cloned.1.call-start = ((), (), s32[]{:S(2)}) async-start(), calls=%async_computation.4 | async-start | bytes 3538944 | tf_op jit(solution)/shard_map/all_gather | solution.py:147
  8.5 23.3 %collective-permute-start.4 = (bf16[512,128]{1,0:T(8,128)(2,1)}, bf16[512,128]{1,0:T(8,128)(2,1)S(1)}, u32[]{:S(2)}, u32[]{:S(2)}) collective-permute-start(bf16[512,128]{1,0:T(8,128)(2,1)} %down_ref.1), channel_id=1, source_target_pairs={{0,384},{1,416},{16,400},{17,432},{32,385},{33,417},{48,401},{49,4... | collective-permute-start | bytes 393224 | tf_op jit(solution)/shard_map/ppermute | solution.py:146
  19.5 12.4 %collective-permute-start.5 = (bf16[512,128]{1,0:T(8,128)(2,1)}, bf16[512,128]{1,0:T(8,128)(2,1)S(1)}, u32[]{:S(2)}, u32[]{:S(2)}) collective-permute-start(bf16[512,128]{1,0:T(8,128)(2,1)} %down_ref.1), channel_id=1, source_target_pairs={{0,256},{1,288},{16,272},{17,304},{32,257},{33,289},{48,273},{49,3... | collective-permute-start | bytes 393224 | tf_op jit(solution)/shard_map/ppermute | solution.py:146
  21.4 10.6 %collective-permute-start.6 = (bf16[512,128]{1,0:T(8,128)(2,1)}, bf16[512,128]{1,0:T(8,128)(2,1)S(1)}, u32[]{:S(2)}, u32[]{:S(2)}) collective-permute-start(bf16[512,128]{1,0:T(8,128)(2,1)} %down_ref.1), channel_id=1, source_target_pairs={{0,128},{1,160},{16,144},{17,176},{32,129},{33,161},{48,145},{49,1... | collective-permute-start | bytes 393224 | tf_op jit(solution)/shard_map/ppermute | solution.py:146
  33.5 9.5 %collective-permute-start = (bf16[128,256]{1,0:T(8,128)(2,1)S(1)}, bf16[128,256]{1,0:T(8,128)(2,1)S(1)}, u32[]{:S(2)}, u32[]{:S(2)}) collective-permute-start(bf16[128,256]{1,0:T(8,128)(2,1)S(1)} %constant_dynamic-slice_fusion), channel_id=1, source_target_pairs={{0,0},{1,1},{2,2},{3,3},{4,128},{5,129},{6,130},{7,131},{8,256},{9... | collective-permute-start | bytes 196616 | tf_op jit(solution)/shard_map/ppermute | solution.py:159
  62.3 3.8 %copy-start.2 = (bf16[8,128,256]{2,1,0:T(8,128)(2,1)}, bf16[8,128,256]{2,1,0:T(8,128)(2,1)S(1)}, u32[]{:S(2)}) copy-start(bf16[8,128,256]{2,1,0:T(8,128)(2,1)S(1)} %all_to_all.15) | copy-start | bytes 1572868
  62.3 3.8 %collective-permute-start.1 = (bf16[4,2,128,256]{3,2,1,0:T(8,128)(2,1)S(1)}, bf16[4,2,128,256]{3,2,1,0:T(8,128)(2,1)S(1)}, u32[]{:S(2)}, u32[]{:S(2)}) collective-permute-start(bf16[4,2,128,256]{3,2,1,0:T(8,128)(2,1)S(1)} %bitcast.44), channel_id=1, source_target_pairs={{0,1},{1,0},{2,3},{3,2},{4,5},{5,4},{6,7},{7,6},{8,9},{9,8},{10,11... | collective-permute-start | bytes 1572872 | tf_op jit(solution)/shard_map/ppermute | solution.py:164
  66.1 0.8 copy-start.4
  66.9 10.1 %copy-start.1 = (bf16[96,128,128]{2,1,0:T(8,128)(2,1)S(1)}, bf16[96,128,128]{2,1,0:T(8,128)(2,1)}, u32[]{:S(2)}) copy-start(bf16[96,128,128]{2,1,0:T(8,128)(2,1)} %all-gather.5.cloned.1.call-done) | copy-start | bytes 9437188
  72.8 25.5 %all-to-all-start.1 = ((bf16[4,128,1024]{2,1,0:T(8,128)(2,1)}), bf16[4,128,1024]{2,1,0:T(8,128)(2,1)}, u32[]{:S(2)}, u32[]{:S(2)}) async-start(bf16[4,128,1024]{2,1,0:T(8,128)(2,1)} %get-tuple-element.13), calls=%async_computation.1 | async-start | bytes 2097152 | tf_op jit(solution)/shard_map/all_to_all | solution.py:172
  77.3 22.7 %collective-permute-start.2 = (bf16[2,2,4,128,128]{4,3,2,1,0:T(8,128)(2,1)S(1)}, bf16[2,2,4,128,128]{4,3,2,1,0:T(8,128)(2,1)S(1)}, u32[]{:S(2)}, u32[]{:S(2)}) collective-permute-start(bf16[2,2,4,128,128]{4,3,2,1,0:T(8,128)(2,1)S(1)} %slice.28), channel_id=1, source_target_pairs={{0,1},{1,0},{2,3},{3,2},{4,5},{5,4},{6,7},{7,6},{8,9},{9,8},{10,11... | collective-permute-start | bytes 1572872 | tf_op jit(solution)/shard_map/ppermute | solution.py:171
  99.9 11.7 %copy-start.3 = (bf16[128,512]{1,0:T(8,128)(2,1)}, bf16[128,512]{1,0:T(8,128)(2,1)S(1)}, u32[]{:S(2)}) copy-start(bf16[128,512]{1,0:T(8,128)(2,1)S(1)} %fusion.mine_ref) | copy-start | bytes 393220
  100.0 11.7 %copy-start.5 = (bf16[2,2,4,128,128]{4,3,2,1,0:T(8,128)(2,1)}, bf16[2,2,4,128,128]{4,3,2,1,0:T(8,128)(2,1)S(1)}, u32[]{:S(2)}) copy-start(bf16[2,2,4,128,128]{4,3,2,1,0:T(8,128)(2,1)S(1)} %collective-permute-done.2.passed_ref) | copy-start | bytes 1572868
  100.0 11.7 %collective-permute-start.3 = (bf16[128,512]{1,0:T(8,128)(2,1)S(1)}, bf16[128,512]{1,0:T(8,128)(2,1)S(1)}, u32[]{:S(2)}, u32[]{:S(2)}) collective-permute-start(bf16[128,512]{1,0:T(8,128)(2,1)S(1)} %fusion.mine_ref), channel_id=1, source_target_pairs={{0,1},{1,0},{2,3},{3,2},{4,5},{5,4},{6,7},{7,6},{8,9},{9,8},{10,11... | collective-permute-start | bytes 393224 | tf_op jit(solution)/shard_map/ppermute | solution.py:180
  111.6 0.6 copy-start.6
  112.3 10.3 %copy-start.8 = (s32[2]{0:T(128)S(1)}, s32[2]{0:T(128)}, u32[]{:S(2)}) copy-start(s32[2]{0:T(128)} %param.10) | copy-start | bytes 28
  112.3 10.3 %copy-start.7 = (s32[256]{0:T(256)S(1)}, s32[256]{0:T(256)}, u32[]{:S(2)}) copy-start(s32[256]{0:T(256)} %param.11) | copy-start | bytes 3076
  116.7 12.7 %all-to-all-start.2 = ((bf16[8,128,256]{2,1,0:T(8,128)(2,1)}), bf16[8,128,256]{2,1,0:T(8,128)(2,1)S(1)}, u32[]{:S(2)}, u32[]{:S(2)}) async-start(bf16[8,128,256]{2,1,0:T(8,128)(2,1)} %bitcast.46), calls=%async_computation.2 | async-start | bytes 1048576 | tf_op jit(solution)/shard_map/all_to_all | solution.py:181
Sparse Core Ops, SparseCore 0:
  9.4 54.7 all-gather.4
  66.3 45.3 all-gather.6

commit v5 on v4

--- a/solution.py
+++ b/solution.py
@@ -10,6 +10,10 @@
 EXP = ("zl", "x", "c")
 F32, BF16 = jnp.float32, jnp.bfloat16
 LANES = 128
+
+
+def in_vmem(array):
+    return pltpu.with_memory_space_constraint(array, pltpu.VMEM)
 
 
 def pack(w_gate, w_up, w_down):
@@ -58,8 +62,8 @@
             num_scalar_prefetch=1,
             grid=(used // 2,),
             in_specs=[
-                pl.BlockSpec(mine.shape, lambda j, s: (0, 0, 0, 0)),
-                pl.BlockSpec(theirs.shape, lambda j, s: (0, 0, 0, 0)),
+                pl.BlockSpec(memory_space=pltpu.VMEM),
+                pl.BlockSpec(memory_space=pltpu.VMEM),
                 pl.BlockSpec((ranks, 2, depth, LANES), lambda j, s: (0, j, 0, 0)),
             ],
             out_specs=[
@@ -82,7 +86,6 @@
     rows, depth = mine.shape
     ranks, others = far.shape[:2]
     groups = others + 1
-    panels = depth // LANES
     quads = ranks // 2
 
     def body(where_ref, mine_ref, theirs_ref, near_ref, passed_ref, far_ref, out_ref):
@@ -92,8 +95,8 @@
             own, other = [], []
             for low in range(2):
                 if s == 0:
-                    own.append(near_ref[core * 2 + low].reshape(depth, LANES))
-                    other.append(passed_ref[0, low].reshape(depth, LANES))
+                    own.append(near_ref[pl.program_id(0) * quads + core * 2 + low].reshape(depth, LANES))
+                    other.append(passed_ref[pl.program_id(0), low].reshape(depth, LANES))
                 else:
                     own.append(far_ref[core * 2 + low, s - 1])
                     other.append(far_ref[(1 - core) * 2 + low, s - 1])
@@ -107,10 +110,10 @@
             num_scalar_prefetch=1,
             grid=(2,),
             in_specs=[
-                pl.BlockSpec(mine.shape, lambda j, s: (0, 0)),
-                pl.BlockSpec(mine.shape, lambda j, s: (0, 0)),
-                pl.BlockSpec((quads, panels) + near.shape[2:], lambda j, s: (j, 2, 0, 0)),
-                pl.BlockSpec((1,) + passed.shape[1:], lambda j, s: (j, 0, 0, 0, 0)),
+                pl.BlockSpec(memory_space=pltpu.VMEM),
+                pl.BlockSpec(memory_space=pltpu.VMEM),
+                pl.BlockSpec(memory_space=pltpu.VMEM),
+                pl.BlockSpec(memory_space=pltpu.VMEM),
                 pl.BlockSpec((quads,) + far.shape[1:], lambda j, s: (j, 0, 0, 0)),
             ],
             out_specs=pl.BlockSpec((groups, 1, rows, 2 * LANES), lambda j, s: (0, j, 0, 0)),
@@ -163,12 +166,12 @@
     mine = mine.reshape(groups, chips // groups, block_rows, width)
     theirs = lax.ppermute(mine, "c", [(0, 1), (1, 0)])
 
-    sent, own = first_product(where, mine, theirs, near)
+    sent, own = first_product(where, in_vmem(mine), in_vmem(theirs), near)
     cores = [(0, 1), (1, 0)]
     later, sent = lax.optimization_barrier((near, sent))
-    later = later.reshape((2, 2, 2) + near.shape[1:])
-    later = lax.dynamic_index_in_dim(later, 1 - core, 1, keepdims=False)[:, :, -(near.shape[1] // 3) :]
-    passed = lax.ppermute(later, "c", cores)
+    later = later[:, -(near.shape[1] // 3) :]
+    other_half = lax.dynamic_index_in_dim(later.reshape((2, 2, 2) + later.shape[1:]), 1 - core, 1, keepdims=False)
+    passed = lax.ppermute(other_half, "c", cores)
     got = lax.all_to_all(sent, "zh", split_axis=0, concat_axis=0, tiled=True)
     total = own
     for k in range(groups):
@@ -177,7 +180,8 @@
     hidden = (jax.nn.silu(gate) * up).astype(BF16)
 
     hidden, passed = lax.optimization_barrier((hidden, passed))
-    part = second_product(where, hidden, lax.ppermute(hidden, "c", cores), near, passed, far)
+    theirs = lax.ppermute(hidden, "c", cores)
+    part = second_product(where, *map(in_vmem, (hidden, theirs, later, passed)), far)
     parts = lax.all_to_all(part.reshape(chips, block_rows, width), ("zl", "x"), split_axis=0, concat_axis=0, tiled=True)
     summed = jnp.sum(parts.astype(F32), 0)
     result = row_scale.reshape(block_count, block_rows, 1) * summed[None]

time: 139 us -> 138 us (level)
  blocking collectives: 19.3 us -> 15.2 us
  waiting for transfers between devices: 45.9 us -> 48.6 us
  starting transfers between devices: 39.7 us -> 41.4 us
  other arithmetic: 4.04 us -> 2.64 us
    all_to_all x1, blocking collectives: 19.3 us -> 15.2 us  [per_device(): lax.all_to_all(copies, ('zl', 'x'), split_axis=0, concat_axis=0, tiled=True)]
    ppermute x3, waiting for transfers between devices: 5.81 us -> 9.07 us  [per_device(): blocks.append(lax.ppermute(w_down, ('zh', 'y', 'c'), moves))]
    all_gather x1, waiting for transfers between devices: 9.73 us -> 12.1 us  [per_device(): far = lax.all_gather(jnp.stack(blocks), 'y', axis=0, tiled=False)]
    all_to_all x1, waiting for transfers between devices: 18.9 us -> 16.6 us  [per_device(): got = lax.all_to_all(sent, 'zh', split_axis=0, concat_axis=0, tiled=True)]
    unnamed x18 -> x8, local copies, waits for them, and re-layouts: 1.5 us -> 0.02 us
where the time goes in v5:
time: 138 us; the launch traced here: 135 us
  waiting for transfers between devices  48.6 us (35%)
  starting transfers between devices  41.4 us (30%)
  blocking collectives  15.2 us (11%)
  between operations  14.2 us (10%)
  Pallas kernels  11 us (8%)
  other arithmetic  2.64 us (2%)
  local copies, waits for them, and re-layouts  2.2 us (2%)
    ppermute x3, starting transfers between devices, per_device(): blocks.append(lax.ppermute(w_down, ('zh', 'y', 'c'), moves))  18.9 us
    all_to_all x1, waiting for transfers between devices, per_device(): got = lax.all_to_all(sent, 'zh', split_axis=0, concat_axis=0, tiled=True)  16.6 us
    all_to_all x1, blocking collectives, per_device(): lax.all_to_all(copies, ('zl', 'x'), split_axis=0, concat_axis=0, tiled=True)  15.2 us
    all_gather x1, waiting for transfers between devices, per_device(): far = lax.all_gather(jnp.stack(blocks), 'y', axis=0, tiled=False)  12.1 us
    ppermute x3, waiting for transfers between devices, per_device(): blocks.append(lax.ppermute(w_down, ('zh', 'y', 'c'), moves))  9.07 us
    all_to_all x1, waiting for transfers between devices, per_device(): lax.all_to_all(part.reshape(chips, block_rows, width), ('zl', 'x'), split...  6.78 us
    ppermute x1, starting transfers between devices, per_device(): rows = lax.ppermute(rows, ('zh',) + EXP, swap)  6.34 us
    all_to_all x1, starting transfers between devices, per_device(): lax.all_to_all(part.reshape(chips, block_rows, width), ('zl', 'x'), split...  5.88 us
  transfers between devices with their start and end apart: 11, of which 7 were waited for; matrix products, arithmetic and copies ran while one was open for 3% of the time, Pallas kernels for 4%

profile of v5, /device:TPU:6, one launch (start us, length us, event | category | flops | bytes accessed | tf_op | source)
XLA Modules:
  0.0 135.3 jit_solution(810861400893140641)
XLA Ops:
  6.5 0.0 copy-start
  6.5 0.0 all-gather.5.cloned.1.call-start
  6.5 1.9 %pack.1 = bf16[12,128,128]{2,1,0:T(8,128)(2,1)} custom-call(bf16[128,512]{1,0:T(8,128)(2,1)} %gate_ref.1, bf16[128,512]{1,0:T(8,128)(2,1)} %up_ref.1, bf16[512,128]{1,0:T(8,128)(2,1)} %down_ref.1), custom_call_target="tpu_custom_call" | custom-call | tf_op jit(solution)/shard_map/pack/pallas_call | solution.py:29
  8.4 0.0 all-gather.5.cloned.1.call-update
  8.4 0.0 all-gather.7.cloned.1.call-start
  8.5 6.1 %collective-permute-start.6 = (bf16[512,128]{1,0:T(8,128)(2,1)}, bf16[512,128]{1,0:T(8,128)(2,1)S(1)}, u32[]{:S(2)}, u32[]{:S(2)}) collective-permute-start(bf16[512,128]{1,0:T(8,128)(2,1)} %down_ref.1), channel_id=1, source_target_pairs={{0,128},{1,160},{16,144},{17,176},{32,129},{33,161},{48,145},{49,1... | collective-permute-start | bytes 393224 | tf_op jit(solution)/shard_map/ppermute | solution.py:149
  14.6 9.1 %collective-permute-start.5 = (bf16[512,128]{1,0:T(8,128)(2,1)}, bf16[512,128]{1,0:T(8,128)(2,1)S(1)}, u32[]{:S(2)}, u32[]{:S(2)}) collective-permute-start(bf16[512,128]{1,0:T(8,128)(2,1)} %down_ref.1), channel_id=1, source_target_pairs={{0,256},{1,288},{16,272},{17,304},{32,257},{33,289},{48,273},{49,3... | collective-permute-start | bytes 393224 | tf_op jit(solution)/shard_map/ppermute | solution.py:149
  23.7 3.7 %collective-permute-start.4 = (bf16[512,128]{1,0:T(8,128)(2,1)}, bf16[512,128]{1,0:T(8,128)(2,1)S(1)}, u32[]{:S(2)}, u32[]{:S(2)}) collective-permute-start(bf16[512,128]{1,0:T(8,128)(2,1)} %down_ref.1), channel_id=1, source_target_pairs={{0,384},{1,416},{16,400},{17,432},{32,385},{33,417},{48,401},{49,4... | collective-permute-start | bytes 393224 | tf_op jit(solution)/shard_map/ppermute | solution.py:149
  27.4 0.0 collective-permute-done.6
  27.4 7.2 %collective-permute-done.5 = bf16[512,128]{1,0:T(8,128)(2,1)S(1)} collective-permute-done((bf16[512,128]{1,0:T(8,128)(2,1)}, bf16[512,128]{1,0:T(8,128)(2,1)S(1)}, u32[]{:S(2)}, u32[]{:S(2)}) %collective-permute-start.5) | collective-permute-done | bytes 131104 | tf_op jit(solution)/shard_map/ppermute | solution.py:149
  34.6 1.9 %collective-permute-done.4 = bf16[512,128]{1,0:T(8,128)(2,1)S(1)} collective-permute-done((bf16[512,128]{1,0:T(8,128)(2,1)}, bf16[512,128]{1,0:T(8,128)(2,1)S(1)}, u32[]{:S(2)}, u32[]{:S(2)}) %collective-permute-start.4) | collective-permute-done | bytes 131104 | tf_op jit(solution)/shard_map/ppermute | solution.py:149
  36.5 0.8 pad_maximum_fusion
  37.3 0.0 all-gather.7.cloned.1.call-update
  38.0 0.0 copy-done
  38.0 6.3 %collective-permute-start = (bf16[128,256]{1,0:T(8,128)(2,1)S(1)}, bf16[128,256]{1,0:T(8,128)(2,1)S(1)}, u32[]{:S(2)}, u32[]{:S(2)}) collective-permute-start(bf16[128,256]{1,0:T(8,128)(2,1)S(1)} %constant_dynamic-slice_fusion), channel_id=1, source_target_pairs={{0,0},{1,1},{2,2},{3,3},{4,128},{5,129},{6,130},{7,131},{8,256},{9... | collective-permute-start | bytes 196616 | tf_op jit(solution)/shard_map/ppermute | solution.py:162
  44.4 3.1 %collective-permute-done = bf16[128,256]{1,0:T(8,128)(2,1)S(1)} collective-permute-done((bf16[128,256]{1,0:T(8,128)(2,1)S(1)}, bf16[128,256]{1,0:T(8,128)(2,1)S(1)}, u32[]{:S(2)}, u32[]{:S(2)}) %collective-permute-start) | collective-permute-done | bytes 65568 | tf_op jit(solution)/shard_map/ppermute | solution.py:162
  47.5 15.2 %all_to_all.15 = bf16[8,128,256]{2,1,0:T(8,128)(2,1)S(1)} all-to-all(bf16[8,128,256]{2,1,0:T(8,128)(2,1)S(1)} %broadcast_in_dim.18), channel_id=1, replica_groups=mesh['zh'=4,'y'=8,'zl'=2,'x'=4,'c'=2] {'zl','x'}, dimensions={0} | all-to-all | bytes 1048576 | tf_op jit(solution)/shard_map/all_to_all | solution.py:165
  62.7 2.5 %collective-permute-start.1 = (bf16[4,2,128,256]{3,2,1,0:T(8,128)(2,1)S(1)}, bf16[4,2,128,256]{3,2,1,0:T(8,128)(2,1)S(1)}, u32[]{:S(2)}, u32[]{:S(2)}) collective-permute-start(bf16[4,2,128,256]{3,2,1,0:T(8,128)(2,1)S(1)} %bitcast.41), channel_id=1, source_target_pairs={{0,1},{1,0},{2,3},{3,2},{4,5},{5,4},{6,7},{7,6},{8,9},{9,8},{10,11... | collective-permute-start | bytes 1572872 | tf_op jit(solution)/shard_map/ppermute | solution.py:167
  65.2 0.6 pad_add_fusion.where_ref
  65.8 0.9 collective-permute-done.1.theirs_ref
  66.7 0.0 all-gather.5.cloned.1.call-done
  66.7 5.3 %first_product.1 = (bf16[4,128,1024]{2,1,0:T(8,128)(2,1)}, f32[128,1024]{1,0:T(8,128)}) custom-call(s32[2]{0:T(128)} %pad_add_fusion.where_ref, bf16[4,2,128,256]{3,2,1,0:T(8,128)(2,1)S(1)} %bitcast.42, bf16[4,2,128,256]{3,2,1,0:T(8,128)(2,1)S(1)} %collective-permute-done.1.theirs_ref, bf16[8,12,128,128]{3,2,1,0:T(8,128)(2,1)} %bitcast.43), custom_call_target="tpu_custom_call" | custom-call | flops 1073741824 | bytes 5242880 | tf_op jit(solution)/shard_map/first_product/pallas_call | solution.py:59
  72.0 0.0 copy-start.1
  72.0 3.6 %all-to-all-start.1 = ((bf16[4,128,1024]{2,1,0:T(8,128)(2,1)}), bf16[4,128,1024]{2,1,0:T(8,128)(2,1)S(1)}, u32[]{:S(2)}, u32[]{:S(2)}) async-start(bf16[4,128,1024]{2,1,0:T(8,128)(2,1)} %get-tuple-element.13), calls=%async_computation.1 | async-start | bytes 2097152 | tf_op jit(solution)/shard_map/all_to_all | solution.py:175
  75.7 1.3 slice.23.near_ref
  77.0 0.8 dynamic-slice_bitcast_fusion
  77.8 2.3 %collective-permute-start.2 = (bf16[2,2,4,128,128]{4,3,2,1,0:T(8,128)(2,1)}, bf16[2,2,4,128,128]{4,3,2,1,0:T(8,128)(2,1)S(1)}, u32[]{:S(2)}, u32[]{:S(2)}) collective-permute-start(bf16[2,2,4,128,128]{4,3,2,1,0:T(8,128)(2,1)} %dynamic-slice_bitcast_fusion), channel_id=1, source_target_pairs={{0,1},{1,0},{2,3},{3,2},{4,5},{5,4},{6,7},{7,6},{8,9},{9,8},{10,11... | collective-permute-start | bytes 1572872 | tf_op jit(solution)/shard_map/ppermute | solution.py:174
  80.1 16.6 %all-to-all-done.1 = bf16[4,128,1024]{2,1,0:T(8,128)(2,1)S(1)} async-done(((bf16[4,128,1024]{2,1,0:T(8,128)(2,1)}), bf16[4,128,1024]{2,1,0:T(8,128)(2,1)S(1)}, u32[]{:S(2)}, u32[]{:S(2)}) %all-to-all-start.1) | async-done | bytes 1048608 | tf_op jit(solution)/shard_map/all_to_all | solution.py:175
  96.7 0.0 copy-done.1
  96.7 0.2 bitcast_add_fusion
  96.9 0.1 fusion.mine_ref
  97.0 0.0 collective-permute-done.2.passed_ref
  97.0 1.9 %collective-permute-start.3 = (bf16[128,512]{1,0:T(8,128)(2,1)S(1)}, bf16[128,512]{1,0:T(8,128)(2,1)S(1)}, u32[]{:S(2)}, u32[]{:S(2)}) collective-permute-start(bf16[128,512]{1,0:T(8,128)(2,1)S(1)} %fusion.mine_ref), channel_id=1, source_target_pairs={{0,1},{1,0},{2,3},{3,2},{4,5},{5,4},{6,7},{7,6},{8,9},{9,8},{10,11... | collective-permute-start | bytes 393224 | tf_op jit(solution)/shard_map/ppermute | solution.py:183
  98.9 12.1 %all-gather.7.cloned.1.call-done = bf16[24,512,128]{2,1,0:T(8,128)(2,1)} async-done(((bf16[3,512,128]{2,1,0:T(8,128)(2,1)}), bf16[24,512,128]{2,1,0:T(8,128)(2,1)}) %all-gather.7.cloned.1.call-update) | async-done | bytes 3145744 | tf_op jit(solution)/shard_map/all_gather | solution.py:150
  111.0 0.0 collective-permute-done.3.theirs_ref
  111.0 0.0 copy-start.3
  111.0 0.0 copy-start.2
  111.0 3.8 %second_product.1 = bf16[4,2,128,256]{3,2,1,0:T(8,128)(2,1)} custom-call(s32[2]{0:T(128)} %pad_add_fusion.where_ref, bf16[128,512]{1,0:T(8,128)(2,1)S(1)} %fusion.mine_ref, bf16[128,512]{1,0:T(8,128)(2,1)S(1)} %collective-permute-done.3.theirs_ref, bf16[8,4,128,128]{3,2,1,0:T(8,128)(2,1)S(1)} %slice.23.near_ref, ...), custom_call_target="tpu_custom_call" | custom-call | flops 536870912 | bytes 5242880 | tf_op jit(solution)/shard_map/second_product/pallas_call | solution.py:107
  114.9 5.9 %all-to-all-start.2 = ((bf16[8,128,256]{2,1,0:T(8,128)(2,1)}), bf16[8,128,256]{2,1,0:T(8,128)(2,1)S(1)}, u32[]{:S(2)}, u32[]{:S(2)}) async-start(bf16[8,128,256]{2,1,0:T(8,128)(2,1)} %bitcast.46), calls=%async_computation.2 | async-start | bytes 1048576 | tf_op jit(solution)/shard_map/all_to_all | solution.py:185
  120.8 0.0 copy-done.3
  120.8 0.0 copy-done.2
  120.8 0.1 fusion.3
  120.9 6.8 %all-to-all-done.2 = bf16[8,128,256]{2,1,0:T(8,128)(2,1)S(1)} async-done(((bf16[8,128,256]{2,1,0:T(8,128)(2,1)}), bf16[8,128,256]{2,1,0:T(8,128)(2,1)S(1)}, u32[]{:S(2)}, u32[]{:S(2)}) %all-to-all-start.2) | async-done | bytes 524320 | tf_op jit(solution)/shard_map/all_to_all | solution.py:185
  127.6 0.1 convert_reduce_fusion
  127.7 0.8 fusion.1
  (3 shorter events, 0.0 us)
Async XLA Ops:
  6.5 31.5 %copy-start = (bf16[256,256]{1,0:T(8,128)(2,1)S(1)}, bf16[256,256]{1,0:T(8,128)(2,1)}, u32[]{:S(2)}) copy-start(bf16[256,256]{1,0:T(8,128)(2,1)} %param.6) | copy-start | bytes 393220
  6.5 60.1 %all-gather.5.cloned.1.call-start = ((), (), s32[]{:S(2)}) async-start(), calls=%async_computation.3 | async-start | bytes 3538944 | tf_op jit(solution)/shard_map/all_gather | solution.py:138
  8.4 102.6 %all-gather.7.cloned.1.call-start = ((), (), s32[]{:S(2)}) async-start(), calls=%async_computation.4 | async-start | bytes 3538944 | tf_op jit(solution)/shard_map/all_gather | solution.py:150
  8.5 18.9 %collective-permute-start.6 = (bf16[512,128]{1,0:T(8,128)(2,1)}, bf16[512,128]{1,0:T(8,128)(2,1)S(1)}, u32[]{:S(2)}, u32[]{:S(2)}) collective-permute-start(bf16[512,128]{1,0:T(8,128)(2,1)} %down_ref.1), channel_id=1, source_target_pairs={{0,128},{1,160},{16,144},{17,176},{32,129},{33,161},{48,145},{49,1... | collective-permute-start | bytes 393224 | tf_op jit(solution)/shard_map/ppermute | solution.py:149
  14.6 20.0 %collective-permute-start.5 = (bf16[512,128]{1,0:T(8,128)(2,1)}, bf16[512,128]{1,0:T(8,128)(2,1)S(1)}, u32[]{:S(2)}, u32[]{:S(2)}) collective-permute-start(bf16[512,128]{1,0:T(8,128)(2,1)} %down_ref.1), channel_id=1, source_target_pairs={{0,256},{1,288},{16,272},{17,304},{32,257},{33,289},{48,273},{49,3... | collective-permute-start | bytes 393224 | tf_op jit(solution)/shard_map/ppermute | solution.py:149
  23.7 12.7 %collective-permute-start.4 = (bf16[512,128]{1,0:T(8,128)(2,1)}, bf16[512,128]{1,0:T(8,128)(2,1)S(1)}, u32[]{:S(2)}, u32[]{:S(2)}) collective-permute-start(bf16[512,128]{1,0:T(8,128)(2,1)} %down_ref.1), channel_id=1, source_target_pairs={{0,384},{1,416},{16,400},{17,432},{32,385},{33,417},{48,401},{49,4... | collective-permute-start | bytes 393224 | tf_op jit(solution)/shard_map/ppermute | solution.py:149
  38.0 9.5 %collective-permute-start = (bf16[128,256]{1,0:T(8,128)(2,1)S(1)}, bf16[128,256]{1,0:T(8,128)(2,1)S(1)}, u32[]{:S(2)}, u32[]{:S(2)}) collective-permute-start(bf16[128,256]{1,0:T(8,128)(2,1)S(1)} %constant_dynamic-slice_fusion), channel_id=1, source_target_pairs={{0,0},{1,1},{2,2},{3,3},{4,128},{5,129},{6,130},{7,131},{8,256},{9... | collective-permute-start | bytes 196616 | tf_op jit(solution)/shard_map/ppermute | solution.py:162
  62.7 4.0 %collective-permute-start.1 = (bf16[4,2,128,256]{3,2,1,0:T(8,128)(2,1)S(1)}, bf16[4,2,128,256]{3,2,1,0:T(8,128)(2,1)S(1)}, u32[]{:S(2)}, u32[]{:S(2)}) collective-permute-start(bf16[4,2,128,256]{3,2,1,0:T(8,128)(2,1)S(1)} %bitcast.41), channel_id=1, source_target_pairs={{0,1},{1,0},{2,3},{3,2},{4,5},{5,4},{6,7},{7,6},{8,9},{9,8},{10,11... | collective-permute-start | bytes 1572872 | tf_op jit(solution)/shard_map/ppermute | solution.py:167
  72.0 24.6 %copy-start.1 = (f32[128,1024]{1,0:T(8,128)S(1)}, f32[128,1024]{1,0:T(8,128)}, u32[]{:S(2)}) copy-start(f32[128,1024]{1,0:T(8,128)} %get-tuple-element.11) | copy-start | bytes 1572868
  72.0 24.6 %all-to-all-start.1 = ((bf16[4,128,1024]{2,1,0:T(8,128)(2,1)}), bf16[4,128,1024]{2,1,0:T(8,128)(2,1)S(1)}, u32[]{:S(2)}, u32[]{:S(2)}) async-start(bf16[4,128,1024]{2,1,0:T(8,128)(2,1)} %get-tuple-element.13), calls=%async_computation.1 | async-start | bytes 2097152 | tf_op jit(solution)/shard_map/all_to_all | solution.py:175
  77.8 19.2 %collective-permute-start.2 = (bf16[2,2,4,128,128]{4,3,2,1,0:T(8,128)(2,1)}, bf16[2,2,4,128,128]{4,3,2,1,0:T(8,128)(2,1)S(1)}, u32[]{:S(2)}, u32[]{:S(2)}) collective-permute-start(bf16[2,2,4,128,128]{4,3,2,1,0:T(8,128)(2,1)} %dynamic-slice_bitcast_fusion), channel_id=1, source_target_pairs={{0,1},{1,0},{2,3},{3,2},{4,5},{5,4},{6,7},{7,6},{8,9},{9,8},{10,11... | collective-permute-start | bytes 1572872 | tf_op jit(solution)/shard_map/ppermute | solution.py:174
  97.0 14.1 %collective-permute-start.3 = (bf16[128,512]{1,0:T(8,128)(2,1)S(1)}, bf16[128,512]{1,0:T(8,128)(2,1)S(1)}, u32[]{:S(2)}, u32[]{:S(2)}) collective-permute-start(bf16[128,512]{1,0:T(8,128)(2,1)S(1)} %fusion.mine_ref), channel_id=1, source_target_pairs={{0,1},{1,0},{2,3},{3,2},{4,5},{5,4},{6,7},{7,6},{8,9},{9,8},{10,11... | collective-permute-start | bytes 393224 | tf_op jit(solution)/shard_map/ppermute | solution.py:183
  111.0 9.7 %copy-start.3 = (s32[2]{0:T(128)S(1)}, s32[2]{0:T(128)}, u32[]{:S(2)}) copy-start(s32[2]{0:T(128)} %param.10) | copy-start | bytes 28
  111.0 9.7 %copy-start.2 = (s32[256]{0:T(256)S(1)}, s32[256]{0:T(256)}, u32[]{:S(2)}) copy-start(s32[256]{0:T(256)} %param.11) | copy-start | bytes 3076
  114.9 12.7 %all-to-all-start.2 = ((bf16[8,128,256]{2,1,0:T(8,128)(2,1)}), bf16[8,128,256]{2,1,0:T(8,128)(2,1)S(1)}, u32[]{:S(2)}, u32[]{:S(2)}) async-start(bf16[8,128,256]{2,1,0:T(8,128)(2,1)} %bitcast.46), calls=%async_computation.2 | async-start | bytes 1048576 | tf_op jit(solution)/shard_map/all_to_all | solution.py:185
Sparse Core Ops, SparseCore 0:
  9.4 55.1 all-gather.4
  66.7 44.3 all-gather.6

commit v6 on v5

--- a/solution.py
+++ b/solution.py
@@ -90,7 +90,7 @@
 
     def body(where_ref, mine_ref, theirs_ref, near_ref, passed_ref, far_ref, out_ref):
         core = where_ref[1]
-        left, right = mine_ref[...], theirs_ref[...]
+        both = jnp.concatenate([mine_ref[...], theirs_ref[...]], 1)
         for s in range(groups):
             own, other = [], []
             for low in range(2):
@@ -100,9 +100,9 @@
                 else:
                     own.append(far_ref[core * 2 + low, s - 1])
                     other.append(far_ref[(1 - core) * 2 + low, s - 1])
-            part = jnp.dot(left, jnp.concatenate(own, 1), preferred_element_type=F32)
-            part = part + jnp.dot(right, jnp.concatenate(other, 1), preferred_element_type=F32)
-            out_ref[lax.rem(where_ref[0] + s, groups), 0] = part.astype(BF16)
+            rhs = jnp.concatenate([jnp.concatenate(own, 1), jnp.concatenate(other, 1)], 0)
+            part = jnp.dot(both, rhs, preferred_element_type=F32)
+            out_ref[lax.rem(where_ref[0] + s, groups), pl.program_id(0)] = part.astype(BF16)
 
     return pl.pallas_call(
         body,
@@ -116,9 +116,9 @@
                 pl.BlockSpec(memory_space=pltpu.VMEM),
                 pl.BlockSpec((quads,) + far.shape[1:], lambda j, s: (j, 0, 0, 0)),
             ],
-            out_specs=pl.BlockSpec((groups, 1, rows, 2 * LANES), lambda j, s: (0, j, 0, 0)),
-        ),
-        out_shape=jax.ShapeDtypeStruct((groups, 2, rows, 2 * LANES), BF16),
+            out_specs=pl.BlockSpec(memory_space=pltpu.VMEM),
+        ),
+        out_shape=pltpu.VMEM((groups, 2, rows, 2 * LANES), BF16),
         cost_estimate=pl.CostEstimate(
             flops=2 * rows * 2 * depth * groups * 4 * LANES, bytes_accessed=5 << 20, transcendentals=0
         ),

time: 138 us -> 138 us (level)
  no operation moved by 1% of the time
where the time goes in v6:
time: 138 us; the launch traced here: 135 us
  waiting for transfers between devices  48.6 us (35%)
  starting transfers between devices  41.4 us (30%)
  blocking collectives  15.2 us (11%)
  between operations  14.2 us (10%)
  Pallas kernels  11.1 us (8%)
  other arithmetic  2.64 us (2%)
  local copies, waits for them, and re-layouts  2.2 us (2%)
    ppermute x3, starting transfers between devices, per_device(): blocks.append(lax.ppermute(w_down, ('zh', 'y', 'c'), moves))  18.9 us
    all_to_all x1, waiting for transfers between devices, per_device(): got = lax.all_to_all(sent, 'zh', split_axis=0, concat_axis=0, tiled=True)  16.6 us
    all_to_all x1, blocking collectives, per_device(): lax.all_to_all(copies, ('zl', 'x'), split_axis=0, concat_axis=0, tiled=True)  15.2 us
    all_gather x1, waiting for transfers between devices, per_device(): far = lax.all_gather(jnp.stack(blocks), 'y', axis=0, tiled=False)  12.1 us
    ppermute x3, waiting for transfers between devices, per_device(): blocks.append(lax.ppermute(w_down, ('zh', 'y', 'c'), moves))  9.07 us
    all_to_all x1, waiting for transfers between devices, per_device(): lax.all_to_all(part.reshape(chips, block_rows, width), ('zl', 'x'), split...  6.78 us
    ppermute x1, starting transfers between devices, per_device(): rows = lax.ppermute(rows, ('zh',) + EXP, swap)  6.34 us
    all_to_all x1, starting transfers between devices, per_device(): lax.all_to_all(part.reshape(chips, block_rows, width), ('zl', 'x'), split...  5.88 us
  transfers between devices with their start and end apart: 11, of which 7 were waited for; matrix products, arithmetic and copies ran while one was open for 3% of the time, Pallas kernels for 4%

profile of v6, /device:TPU:6, one launch (start us, length us, event | category | flops | bytes accessed | tf_op | source)
XLA Modules:
  0.0 135.4 jit_solution(16607368630961223934)
XLA Ops:
  6.5 0.0 copy-start
  6.5 0.0 all-gather.5.cloned.1.call-start
  6.5 1.9 %pack.1 = bf16[12,128,128]{2,1,0:T(8,128)(2,1)} custom-call(bf16[128,512]{1,0:T(8,128)(2,1)} %gate_ref.1, bf16[128,512]{1,0:T(8,128)(2,1)} %up_ref.1, bf16[512,128]{1,0:T(8,128)(2,1)} %down_ref.1), custom_call_target="tpu_custom_call" | custom-call | tf_op jit(solution)/shard_map/pack/pallas_call | solution.py:29
  8.4 0.0 all-gather.5.cloned.1.call-update
  8.4 0.0 all-gather.7.cloned.1.call-start
  8.5 6.1 %collective-permute-start.6 = (bf16[512,128]{1,0:T(8,128)(2,1)}, bf16[512,128]{1,0:T(8,128)(2,1)S(1)}, u32[]{:S(2)}, u32[]{:S(2)}) collective-permute-start(bf16[512,128]{1,0:T(8,128)(2,1)} %down_ref.1), channel_id=1, source_target_pairs={{0,128},{1,160},{16,144},{17,176},{32,129},{33,161},{48,145},{49,1... | collective-permute-start | bytes 393224 | tf_op jit(solution)/shard_map/ppermute | solution.py:149
  14.6 9.1 %collective-permute-start.5 = (bf16[512,128]{1,0:T(8,128)(2,1)}, bf16[512,128]{1,0:T(8,128)(2,1)S(1)}, u32[]{:S(2)}, u32[]{:S(2)}) collective-permute-start(bf16[512,128]{1,0:T(8,128)(2,1)} %down_ref.1), channel_id=1, source_target_pairs={{0,256},{1,288},{16,272},{17,304},{32,257},{33,289},{48,273},{49,3... | collective-permute-start | bytes 393224 | tf_op jit(solution)/shard_map/ppermute | solution.py:149
  23.7 3.7 %collective-permute-start.4 = (bf16[512,128]{1,0:T(8,128)(2,1)}, bf16[512,128]{1,0:T(8,128)(2,1)S(1)}, u32[]{:S(2)}, u32[]{:S(2)}) collective-permute-start(bf16[512,128]{1,0:T(8,128)(2,1)} %down_ref.1), channel_id=1, source_target_pairs={{0,384},{1,416},{16,400},{17,432},{32,385},{33,417},{48,401},{49,4... | collective-permute-start | bytes 393224 | tf_op jit(solution)/shard_map/ppermute | solution.py:149
  27.4 0.0 collective-permute-done.6
  27.4 7.2 %collective-permute-done.5 = bf16[512,128]{1,0:T(8,128)(2,1)S(1)} collective-permute-done((bf16[512,128]{1,0:T(8,128)(2,1)}, bf16[512,128]{1,0:T(8,128)(2,1)S(1)}, u32[]{:S(2)}, u32[]{:S(2)}) %collective-permute-start.5) | collective-permute-done | bytes 131104 | tf_op jit(solution)/shard_map/ppermute | solution.py:149
  34.6 1.9 %collective-permute-done.4 = bf16[512,128]{1,0:T(8,128)(2,1)S(1)} collective-permute-done((bf16[512,128]{1,0:T(8,128)(2,1)}, bf16[512,128]{1,0:T(8,128)(2,1)S(1)}, u32[]{:S(2)}, u32[]{:S(2)}) %collective-permute-start.4) | collective-permute-done | bytes 131104 | tf_op jit(solution)/shard_map/ppermute | solution.py:149
  36.5 0.8 pad_maximum_fusion
  37.3 0.0 all-gather.7.cloned.1.call-update
  38.0 0.0 copy-done
  38.0 6.3 %collective-permute-start = (bf16[128,256]{1,0:T(8,128)(2,1)S(1)}, bf16[128,256]{1,0:T(8,128)(2,1)S(1)}, u32[]{:S(2)}, u32[]{:S(2)}) collective-permute-start(bf16[128,256]{1,0:T(8,128)(2,1)S(1)} %constant_dynamic-slice_fusion), channel_id=1, source_target_pairs={{0,0},{1,1},{2,2},{3,3},{4,128},{5,129},{6,130},{7,131},{8,256},{9... | collective-permute-start | bytes 196616 | tf_op jit(solution)/shard_map/ppermute | solution.py:162
  44.4 3.1 %collective-permute-done = bf16[128,256]{1,0:T(8,128)(2,1)S(1)} collective-permute-done((bf16[128,256]{1,0:T(8,128)(2,1)S(1)}, bf16[128,256]{1,0:T(8,128)(2,1)S(1)}, u32[]{:S(2)}, u32[]{:S(2)}) %collective-permute-start) | collective-permute-done | bytes 65568 | tf_op jit(solution)/shard_map/ppermute | solution.py:162
  47.5 15.2 %all_to_all.15 = bf16[8,128,256]{2,1,0:T(8,128)(2,1)S(1)} all-to-all(bf16[8,128,256]{2,1,0:T(8,128)(2,1)S(1)} %broadcast_in_dim.18), channel_id=1, replica_groups=mesh['zh'=4,'y'=8,'zl'=2,'x'=4,'c'=2] {'zl','x'}, dimensions={0} | all-to-all | bytes 1048576 | tf_op jit(solution)/shard_map/all_to_all | solution.py:165
  62.7 2.5 %collective-permute-start.1 = (bf16[4,2,128,256]{3,2,1,0:T(8,128)(2,1)S(1)}, bf16[4,2,128,256]{3,2,1,0:T(8,128)(2,1)S(1)}, u32[]{:S(2)}, u32[]{:S(2)}) collective-permute-start(bf16[4,2,128,256]{3,2,1,0:T(8,128)(2,1)S(1)} %bitcast.41), channel_id=1, source_target_pairs={{0,1},{1,0},{2,3},{3,2},{4,5},{5,4},{6,7},{7,6},{8,9},{9,8},{10,11... | collective-permute-start | bytes 1572872 | tf_op jit(solution)/shard_map/ppermute | solution.py:167
  65.2 0.6 pad_add_fusion.where_ref
  65.8 0.9 collective-permute-done.1.theirs_ref
  66.7 0.0 all-gather.5.cloned.1.call-done
  66.7 5.3 %first_product.1 = (bf16[4,128,1024]{2,1,0:T(8,128)(2,1)}, f32[128,1024]{1,0:T(8,128)}) custom-call(s32[2]{0:T(128)} %pad_add_fusion.where_ref, bf16[4,2,128,256]{3,2,1,0:T(8,128)(2,1)S(1)} %bitcast.42, bf16[4,2,128,256]{3,2,1,0:T(8,128)(2,1)S(1)} %collective-permute-done.1.theirs_ref, bf16[8,12,128,128]{3,2,1,0:T(8,128)(2,1)} %bitcast.43), custom_call_target="tpu_custom_call" | custom-call | flops 1073741824 | bytes 5242880 | tf_op jit(solution)/shard_map/first_product/pallas_call | solution.py:59
  72.0 0.0 copy-start.1
  72.0 3.6 %all-to-all-start.1 = ((bf16[4,128,1024]{2,1,0:T(8,128)(2,1)}), bf16[4,128,1024]{2,1,0:T(8,128)(2,1)S(1)}, u32[]{:S(2)}, u32[]{:S(2)}) async-start(bf16[4,128,1024]{2,1,0:T(8,128)(2,1)} %get-tuple-element.13), calls=%async_computation.1 | async-start | bytes 2097152 | tf_op jit(solution)/shard_map/all_to_all | solution.py:175
  75.7 1.3 slice.23.near_ref
  77.0 0.8 dynamic-slice_bitcast_fusion
  77.8 2.3 %collective-permute-start.2 = (bf16[2,2,4,128,128]{4,3,2,1,0:T(8,128)(2,1)}, bf16[2,2,4,128,128]{4,3,2,1,0:T(8,128)(2,1)S(1)}, u32[]{:S(2)}, u32[]{:S(2)}) collective-permute-start(bf16[2,2,4,128,128]{4,3,2,1,0:T(8,128)(2,1)} %dynamic-slice_bitcast_fusion), channel_id=1, source_target_pairs={{0,1},{1,0},{2,3},{3,2},{4,5},{5,4},{6,7},{7,6},{8,9},{9,8},{10,11... | collective-permute-start | bytes 1572872 | tf_op jit(solution)/shard_map/ppermute | solution.py:174
  80.1 16.6 %all-to-all-done.1 = bf16[4,128,1024]{2,1,0:T(8,128)(2,1)S(1)} async-done(((bf16[4,128,1024]{2,1,0:T(8,128)(2,1)}), bf16[4,128,1024]{2,1,0:T(8,128)(2,1)S(1)}, u32[]{:S(2)}, u32[]{:S(2)}) %all-to-all-start.1) | async-done | bytes 1048608 | tf_op jit(solution)/shard_map/all_to_all | solution.py:175
  96.7 0.0 copy-done.1
  96.7 0.2 bitcast_add_fusion
  96.9 0.1 fusion.mine_ref
  97.0 0.0 collective-permute-done.2.passed_ref
  97.0 1.9 %collective-permute-start.3 = (bf16[128,512]{1,0:T(8,128)(2,1)S(1)}, bf16[128,512]{1,0:T(8,128)(2,1)S(1)}, u32[]{:S(2)}, u32[]{:S(2)}) collective-permute-start(bf16[128,512]{1,0:T(8,128)(2,1)S(1)} %fusion.mine_ref), channel_id=1, source_target_pairs={{0,1},{1,0},{2,3},{3,2},{4,5},{5,4},{6,7},{7,6},{8,9},{9,8},{10,11... | collective-permute-start | bytes 393224 | tf_op jit(solution)/shard_map/ppermute | solution.py:183
  98.9 12.1 %all-gather.7.cloned.1.call-done = bf16[24,512,128]{2,1,0:T(8,128)(2,1)} async-done(((bf16[3,512,128]{2,1,0:T(8,128)(2,1)}), bf16[24,512,128]{2,1,0:T(8,128)(2,1)}) %all-gather.7.cloned.1.call-update) | async-done | bytes 3145744 | tf_op jit(solution)/shard_map/all_gather | solution.py:150
  111.0 0.0 collective-permute-done.3.theirs_ref
  111.0 0.0 copy-start.3
  111.0 0.0 copy-start.2
  111.0 3.9 %second_product.1 = bf16[4,2,128,256]{3,2,1,0:T(8,128)(2,1)} custom-call(s32[2]{0:T(128)} %pad_add_fusion.where_ref, bf16[128,512]{1,0:T(8,128)(2,1)S(1)} %fusion.mine_ref, bf16[128,512]{1,0:T(8,128)(2,1)S(1)} %collective-permute-done.3.theirs_ref, bf16[8,4,128,128]{3,2,1,0:T(8,128)(2,1)S(1)} %slice.23.near_ref, ...), custom_call_target="tpu_custom_call" | custom-call | flops 536870912 | bytes 5242880 | tf_op jit(solution)/shard_map/second_product/pallas_call | solution.py:107
  115.0 5.9 %all-to-all-start.2 = ((bf16[8,128,256]{2,1,0:T(8,128)(2,1)}), bf16[8,128,256]{2,1,0:T(8,128)(2,1)S(1)}, u32[]{:S(2)}, u32[]{:S(2)}) async-start(bf16[8,128,256]{2,1,0:T(8,128)(2,1)} %bitcast.16), calls=%async_computation.2 | async-start | bytes 1048576 | tf_op jit(solution)/shard_map/all_to_all | solution.py:185
  120.9 0.0 copy-done.3
  120.9 0.0 copy-done.2
  120.9 0.1 fusion.3
  120.9 6.8 %all-to-all-done.2 = bf16[8,128,256]{2,1,0:T(8,128)(2,1)S(1)} async-done(((bf16[8,128,256]{2,1,0:T(8,128)(2,1)}), bf16[8,128,256]{2,1,0:T(8,128)(2,1)S(1)}, u32[]{:S(2)}, u32[]{:S(2)}) %all-to-all-start.2) | async-done | bytes 524320 | tf_op jit(solution)/shard_map/all_to_all | solution.py:185
  127.7 0.1 convert_reduce_fusion
  127.8 0.8 fusion.1
  (3 shorter events, 0.0 us)
Async XLA Ops:
  6.5 31.5 %copy-start = (bf16[256,256]{1,0:T(8,128)(2,1)S(1)}, bf16[256,256]{1,0:T(8,128)(2,1)}, u32[]{:S(2)}) copy-start(bf16[256,256]{1,0:T(8,128)(2,1)} %param.6) | copy-start | bytes 393220
  6.5 60.1 %all-gather.5.cloned.1.call-start = ((), (), s32[]{:S(2)}) async-start(), calls=%async_computation.3 | async-start | bytes 3538944 | tf_op jit(solution)/shard_map/all_gather | solution.py:138
  8.4 102.6 %all-gather.7.cloned.1.call-start = ((), (), s32[]{:S(2)}) async-start(), calls=%async_computation.4 | async-start | bytes 3538944 | tf_op jit(solution)/shard_map/all_gather | solution.py:150
  8.5 18.9 %collective-permute-start.6 = (bf16[512,128]{1,0:T(8,128)(2,1)}, bf16[512,128]{1,0:T(8,128)(2,1)S(1)}, u32[]{:S(2)}, u32[]{:S(2)}) collective-permute-start(bf16[512,128]{1,0:T(8,128)(2,1)} %down_ref.1), channel_id=1, source_target_pairs={{0,128},{1,160},{16,144},{17,176},{32,129},{33,161},{48,145},{49,1... | collective-permute-start | bytes 393224 | tf_op jit(solution)/shard_map/ppermute | solution.py:149
  14.6 20.0 %collective-permute-start.5 = (bf16[512,128]{1,0:T(8,128)(2,1)}, bf16[512,128]{1,0:T(8,128)(2,1)S(1)}, u32[]{:S(2)}, u32[]{:S(2)}) collective-permute-start(bf16[512,128]{1,0:T(8,128)(2,1)} %down_ref.1), channel_id=1, source_target_pairs={{0,256},{1,288},{16,272},{17,304},{32,257},{33,289},{48,273},{49,3... | collective-permute-start | bytes 393224 | tf_op jit(solution)/shard_map/ppermute | solution.py:149
  23.7 12.7 %collective-permute-start.4 = (bf16[512,128]{1,0:T(8,128)(2,1)}, bf16[512,128]{1,0:T(8,128)(2,1)S(1)}, u32[]{:S(2)}, u32[]{:S(2)}) collective-permute-start(bf16[512,128]{1,0:T(8,128)(2,1)} %down_ref.1), channel_id=1, source_target_pairs={{0,384},{1,416},{16,400},{17,432},{32,385},{33,417},{48,401},{49,4... | collective-permute-start | bytes 393224 | tf_op jit(solution)/shard_map/ppermute | solution.py:149
  38.0 9.5 %collective-permute-start = (bf16[128,256]{1,0:T(8,128)(2,1)S(1)}, bf16[128,256]{1,0:T(8,128)(2,1)S(1)}, u32[]{:S(2)}, u32[]{:S(2)}) collective-permute-start(bf16[128,256]{1,0:T(8,128)(2,1)S(1)} %constant_dynamic-slice_fusion), channel_id=1, source_target_pairs={{0,0},{1,1},{2,2},{3,3},{4,128},{5,129},{6,130},{7,131},{8,256},{9... | collective-permute-start | bytes 196616 | tf_op jit(solution)/shard_map/ppermute | solution.py:162
  62.7 4.0 %collective-permute-start.1 = (bf16[4,2,128,256]{3,2,1,0:T(8,128)(2,1)S(1)}, bf16[4,2,128,256]{3,2,1,0:T(8,128)(2,1)S(1)}, u32[]{:S(2)}, u32[]{:S(2)}) collective-permute-start(bf16[4,2,128,256]{3,2,1,0:T(8,128)(2,1)S(1)} %bitcast.41), channel_id=1, source_target_pairs={{0,1},{1,0},{2,3},{3,2},{4,5},{5,4},{6,7},{7,6},{8,9},{9,8},{10,11... | collective-permute-start | bytes 1572872 | tf_op jit(solution)/shard_map/ppermute | solution.py:167
  72.0 24.6 %copy-start.1 = (f32[128,1024]{1,0:T(8,128)S(1)}, f32[128,1024]{1,0:T(8,128)}, u32[]{:S(2)}) copy-start(f32[128,1024]{1,0:T(8,128)} %get-tuple-element.11) | copy-start | bytes 1572868
  72.0 24.6 %all-to-all-start.1 = ((bf16[4,128,1024]{2,1,0:T(8,128)(2,1)}), bf16[4,128,1024]{2,1,0:T(8,128)(2,1)S(1)}, u32[]{:S(2)}, u32[]{:S(2)}) async-start(bf16[4,128,1024]{2,1,0:T(8,128)(2,1)} %get-tuple-element.13), calls=%async_computation.1 | async-start | bytes 2097152 | tf_op jit(solution)/shard_map/all_to_all | solution.py:175
  77.8 19.2 %collective-permute-start.2 = (bf16[2,2,4,128,128]{4,3,2,1,0:T(8,128)(2,1)}, bf16[2,2,4,128,128]{4,3,2,1,0:T(8,128)(2,1)S(1)}, u32[]{:S(2)}, u32[]{:S(2)}) collective-permute-start(bf16[2,2,4,128,128]{4,3,2,1,0:T(8,128)(2,1)} %dynamic-slice_bitcast_fusion), channel_id=1, source_target_pairs={{0,1},{1,0},{2,3},{3,2},{4,5},{5,4},{6,7},{7,6},{8,9},{9,8},{10,11... | collective-permute-start | bytes 1572872 | tf_op jit(solution)/shard_map/ppermute | solution.py:174
  97.0 14.1 %collective-permute-start.3 = (bf16[128,512]{1,0:T(8,128)(2,1)S(1)}, bf16[128,512]{1,0:T(8,128)(2,1)S(1)}, u32[]{:S(2)}, u32[]{:S(2)}) collective-permute-start(bf16[128,512]{1,0:T(8,128)(2,1)S(1)} %fusion.mine_ref), channel_id=1, source_target_pairs={{0,1},{1,0},{2,3},{3,2},{4,5},{5,4},{6,7},{7,6},{8,9},{9,8},{10,11... | collective-permute-start | bytes 393224 | tf_op jit(solution)/shard_map/ppermute | solution.py:183
  111.0 9.8 %copy-start.3 = (s32[2]{0:T(128)S(1)}, s32[2]{0:T(128)}, u32[]{:S(2)}) copy-start(s32[2]{0:T(128)} %param.10) | copy-start | bytes 28
  111.0 9.8 %copy-start.2 = (s32[256]{0:T(256)S(1)}, s32[256]{0:T(256)}, u32[]{:S(2)}) copy-start(s32[256]{0:T(256)} %param.11) | copy-start | bytes 3076
  115.0 12.7 %all-to-all-start.2 = ((bf16[8,128,256]{2,1,0:T(8,128)(2,1)}), bf16[8,128,256]{2,1,0:T(8,128)(2,1)S(1)}, u32[]{:S(2)}, u32[]{:S(2)}) async-start(bf16[8,128,256]{2,1,0:T(8,128)(2,1)} %bitcast.16), calls=%async_computation.2 | async-start | bytes 1048576 | tf_op jit(solution)/shard_map/all_to_all | solution.py:185
Sparse Core Ops, SparseCore 0:
  9.4 55.1 all-gather.4
  66.7 44.3 all-gather.6

commit v7 on v6

--- a/solution.py
+++ b/solution.py
@@ -20,15 +20,34 @@
     rows, cols = w_gate.shape
     panels = cols // LANES
 
-    def body(gate_ref, up_ref, down_ref, out_ref):
+    def body(gate_ref, up_ref, down_ref, out_ref, held_ref, in_sems, out_sems):
+        loads = []
         for j in range(panels):
-            out_ref[j] = gate_ref[:, j * LANES : (j + 1) * LANES]
-            out_ref[panels + j] = up_ref[:, j * LANES : (j + 1) * LANES]
-            out_ref[2 * panels + j] = down_ref[j * rows : (j + 1) * rows]
+            at = pl.ds(j * LANES, LANES)
+            for part, source in enumerate((gate_ref.at[:, at], up_ref.at[:, at], down_ref.at[pl.ds(j * rows, rows)])):
+                k = part * panels + j
+                loads.append((k, pltpu.make_async_copy(source, held_ref.at[k], in_sems.at[k])))
+        for _, load in loads:
+            load.start()
+        stores = []
+        for k, load in loads:
+            load.wait()
+            store = pltpu.make_async_copy(held_ref.at[k], out_ref.at[k], out_sems.at[k])
+            store.start()
+            stores.append(store)
+        for store in stores:
+            store.wait()
 
     return pl.pallas_call(
         body,
+        in_specs=[pl.BlockSpec(memory_space=pl.ANY)] * 3,
+        out_specs=pl.BlockSpec(memory_space=pl.ANY),
         out_shape=jax.ShapeDtypeStruct((3 * panels, rows, LANES), BF16),
+        scratch_shapes=[
+            pltpu.VMEM((3 * panels, rows, LANES), BF16),
+            pltpu.SemaphoreType.DMA((3 * panels,)),
+            pltpu.SemaphoreType.DMA((3 * panels,)),
+        ],
         name="pack",
     )(w_gate, w_up, w_down)
 

time: 138 us -> 138 us (level)
  no operation moved by 1% of the time
where the time goes in v7:
time: 138 us; the launch traced here: 135 us
  waiting for transfers between devices  48.7 us (35%)
  starting transfers between devices  41.2 us (30%)
  blocking collectives  15.4 us (11%)
  between operations  14.2 us (10%)
  Pallas kernels  11 us (8%)
  other arithmetic  2.64 us (2%)
  local copies, waits for them, and re-layouts  2.2 us (2%)
    ppermute x3, starting transfers between devices, per_device(): blocks.append(lax.ppermute(w_down, ('zh', 'y', 'c'), moves))  18.9 us
    all_to_all x1, waiting for transfers between devices, per_device(): got = lax.all_to_all(sent, 'zh', split_axis=0, concat_axis=0, tiled=True)  16.7 us
    all_to_all x1, blocking collectives, per_device(): lax.all_to_all(copies, ('zl', 'x'), split_axis=0, concat_axis=0, tiled=True)  15.4 us
    all_gather x1, waiting for transfers between devices, per_device(): far = lax.all_gather(jnp.stack(blocks), 'y', axis=0, tiled=False)  12 us
    ppermute x3, waiting for transfers between devices, per_device(): blocks.append(lax.ppermute(w_down, ('zh', 'y', 'c'), moves))  9.15 us
    all_to_all x1, waiting for transfers between devices, per_device(): lax.all_to_all(part.reshape(chips, block_rows, width), ('zl', 'x'), split...  6.77 us
    ppermute x1, starting transfers between devices, per_device(): rows = lax.ppermute(rows, ('zh',) + EXP, swap)  6.23 us
    all_to_all x1, starting transfers between devices, per_device(): lax.all_to_all(part.reshape(chips, block_rows, width), ('zl', 'x'), split...  5.88 us
  transfers between devices with their start and end apart: 11, of which 7 were waited for; matrix products, arithmetic and copies ran while one was open for 3% of the time, Pallas kernels for 4%

profile of v7, /device:TPU:6, one launch (start us, length us, event | category | flops | bytes accessed | tf_op | source)
XLA Modules:
  0.0 135.3 jit_solution(14365038802377952917)
XLA Ops:
  6.5 0.0 copy-start
  6.5 0.0 all-gather.5.cloned.1.call-start
  6.5 1.8 %pack.1 = bf16[12,128,128]{2,1,0:T(8,128)(2,1)} custom-call(bf16[128,512]{1,0:T(8,128)(2,1)} %gate_ref.1, bf16[128,512]{1,0:T(8,128)(2,1)} %up_ref.1, bf16[512,128]{1,0:T(8,128)(2,1)} %down_ref.1), custom_call_target="tpu_custom_call" | custom-call | tf_op jit(solution)/shard_map/pack/pallas_call | solution.py:41
  8.3 0.0 all-gather.5.cloned.1.call-update
  8.4 0.0 all-gather.7.cloned.1.call-start
  8.4 6.1 %collective-permute-start.6 = (bf16[512,128]{1,0:T(8,128)(2,1)}, bf16[512,128]{1,0:T(8,128)(2,1)S(1)}, u32[]{:S(2)}, u32[]{:S(2)}) collective-permute-start(bf16[512,128]{1,0:T(8,128)(2,1)} %down_ref.1), channel_id=1, source_target_pairs={{0,128},{1,160},{16,144},{17,176},{32,129},{33,161},{48,145},{49,1... | collective-permute-start | bytes 393224 | tf_op jit(solution)/shard_map/ppermute | solution.py:168
  14.5 9.1 %collective-permute-start.5 = (bf16[512,128]{1,0:T(8,128)(2,1)}, bf16[512,128]{1,0:T(8,128)(2,1)S(1)}, u32[]{:S(2)}, u32[]{:S(2)}) collective-permute-start(bf16[512,128]{1,0:T(8,128)(2,1)} %down_ref.1), channel_id=1, source_target_pairs={{0,256},{1,288},{16,272},{17,304},{32,257},{33,289},{48,273},{49,3... | collective-permute-start | bytes 393224 | tf_op jit(solution)/shard_map/ppermute | solution.py:168
  23.6 3.7 %collective-permute-start.4 = (bf16[512,128]{1,0:T(8,128)(2,1)}, bf16[512,128]{1,0:T(8,128)(2,1)S(1)}, u32[]{:S(2)}, u32[]{:S(2)}) collective-permute-start(bf16[512,128]{1,0:T(8,128)(2,1)} %down_ref.1), channel_id=1, source_target_pairs={{0,384},{1,416},{16,400},{17,432},{32,385},{33,417},{48,401},{49,4... | collective-permute-start | bytes 393224 | tf_op jit(solution)/shard_map/ppermute | solution.py:168
  27.3 0.0 collective-permute-done.6
  27.3 7.2 %collective-permute-done.5 = bf16[512,128]{1,0:T(8,128)(2,1)S(1)} collective-permute-done((bf16[512,128]{1,0:T(8,128)(2,1)}, bf16[512,128]{1,0:T(8,128)(2,1)S(1)}, u32[]{:S(2)}, u32[]{:S(2)}) %collective-permute-start.5) | collective-permute-done | bytes 131104 | tf_op jit(solution)/shard_map/ppermute | solution.py:168
  34.5 2.0 %collective-permute-done.4 = bf16[512,128]{1,0:T(8,128)(2,1)S(1)} collective-permute-done((bf16[512,128]{1,0:T(8,128)(2,1)}, bf16[512,128]{1,0:T(8,128)(2,1)S(1)}, u32[]{:S(2)}, u32[]{:S(2)}) %collective-permute-start.4) | collective-permute-done | bytes 131104 | tf_op jit(solution)/shard_map/ppermute | solution.py:168
  36.5 0.8 pad_maximum_fusion
  37.3 0.0 all-gather.7.cloned.1.call-update
  38.0 0.0 copy-done
  38.0 6.2 %collective-permute-start = (bf16[128,256]{1,0:T(8,128)(2,1)S(1)}, bf16[128,256]{1,0:T(8,128)(2,1)S(1)}, u32[]{:S(2)}, u32[]{:S(2)}) collective-permute-start(bf16[128,256]{1,0:T(8,128)(2,1)S(1)} %constant_dynamic-slice_fusion), channel_id=1, source_target_pairs={{0,0},{1,1},{2,2},{3,3},{4,128},{5,129},{6,130},{7,131},{8,256},{9... | collective-permute-start | bytes 196616 | tf_op jit(solution)/shard_map/ppermute | solution.py:181
  44.3 3.2 %collective-permute-done = bf16[128,256]{1,0:T(8,128)(2,1)S(1)} collective-permute-done((bf16[128,256]{1,0:T(8,128)(2,1)S(1)}, bf16[128,256]{1,0:T(8,128)(2,1)S(1)}, u32[]{:S(2)}, u32[]{:S(2)}) %collective-permute-start) | collective-permute-done | bytes 65568 | tf_op jit(solution)/shard_map/ppermute | solution.py:181
  47.5 15.4 %all_to_all.15 = bf16[8,128,256]{2,1,0:T(8,128)(2,1)S(1)} all-to-all(bf16[8,128,256]{2,1,0:T(8,128)(2,1)S(1)} %broadcast_in_dim.18), channel_id=1, replica_groups=mesh['zh'=4,'y'=8,'zl'=2,'x'=4,'c'=2] {'zl','x'}, dimensions={0} | all-to-all | bytes 1048576 | tf_op jit(solution)/shard_map/all_to_all | solution.py:184
  62.9 2.3 %collective-permute-start.1 = (bf16[4,2,128,256]{3,2,1,0:T(8,128)(2,1)S(1)}, bf16[4,2,128,256]{3,2,1,0:T(8,128)(2,1)S(1)}, u32[]{:S(2)}, u32[]{:S(2)}) collective-permute-start(bf16[4,2,128,256]{3,2,1,0:T(8,128)(2,1)S(1)} %bitcast.41), channel_id=1, source_target_pairs={{0,1},{1,0},{2,3},{3,2},{4,5},{5,4},{6,7},{7,6},{8,9},{9,8},{10,11... | collective-permute-start | bytes 1572872 | tf_op jit(solution)/shard_map/ppermute | solution.py:186
  65.2 0.6 pad_add_fusion.where_ref
  65.8 0.9 collective-permute-done.1.theirs_ref
  66.7 0.0 all-gather.5.cloned.1.call-done
  66.7 5.3 %first_product.1 = (bf16[4,128,1024]{2,1,0:T(8,128)(2,1)}, f32[128,1024]{1,0:T(8,128)}) custom-call(s32[2]{0:T(128)} %pad_add_fusion.where_ref, bf16[4,2,128,256]{3,2,1,0:T(8,128)(2,1)S(1)} %bitcast.42, bf16[4,2,128,256]{3,2,1,0:T(8,128)(2,1)S(1)} %collective-permute-done.1.theirs_ref, bf16[8,12,128,128]{3,2,1,0:T(8,128)(2,1)} %bitcast.43), custom_call_target="tpu_custom_call" | custom-call | flops 1073741824 | bytes 5242880 | tf_op jit(solution)/shard_map/first_product/pallas_call | solution.py:78
  72.0 0.0 copy-start.1
  72.0 3.6 %all-to-all-start.1 = ((bf16[4,128,1024]{2,1,0:T(8,128)(2,1)}), bf16[4,128,1024]{2,1,0:T(8,128)(2,1)S(1)}, u32[]{:S(2)}, u32[]{:S(2)}) async-start(bf16[4,128,1024]{2,1,0:T(8,128)(2,1)} %get-tuple-element.13), calls=%async_computation.1 | async-start | bytes 2097152 | tf_op jit(solution)/shard_map/all_to_all | solution.py:194
  75.7 1.3 slice.23.near_ref
  77.0 0.8 dynamic-slice_bitcast_fusion
  77.8 2.3 %collective-permute-start.2 = (bf16[2,2,4,128,128]{4,3,2,1,0:T(8,128)(2,1)}, bf16[2,2,4,128,128]{4,3,2,1,0:T(8,128)(2,1)S(1)}, u32[]{:S(2)}, u32[]{:S(2)}) collective-permute-start(bf16[2,2,4,128,128]{4,3,2,1,0:T(8,128)(2,1)} %dynamic-slice_bitcast_fusion), channel_id=1, source_target_pairs={{0,1},{1,0},{2,3},{3,2},{4,5},{5,4},{6,7},{7,6},{8,9},{9,8},{10,11... | collective-permute-start | bytes 1572872 | tf_op jit(solution)/shard_map/ppermute | solution.py:193
  80.1 16.7 %all-to-all-done.1 = bf16[4,128,1024]{2,1,0:T(8,128)(2,1)S(1)} async-done(((bf16[4,128,1024]{2,1,0:T(8,128)(2,1)}), bf16[4,128,1024]{2,1,0:T(8,128)(2,1)S(1)}, u32[]{:S(2)}, u32[]{:S(2)}) %all-to-all-start.1) | async-done | bytes 1048608 | tf_op jit(solution)/shard_map/all_to_all | solution.py:194
  96.8 0.0 copy-done.1
  96.8 0.2 bitcast_add_fusion
  97.0 0.1 fusion.mine_ref
  97.1 0.0 collective-permute-done.2.passed_ref
  97.1 1.9 %collective-permute-start.3 = (bf16[128,512]{1,0:T(8,128)(2,1)S(1)}, bf16[128,512]{1,0:T(8,128)(2,1)S(1)}, u32[]{:S(2)}, u32[]{:S(2)}) collective-permute-start(bf16[128,512]{1,0:T(8,128)(2,1)S(1)} %fusion.mine_ref), channel_id=1, source_target_pairs={{0,1},{1,0},{2,3},{3,2},{4,5},{5,4},{6,7},{7,6},{8,9},{9,8},{10,11... | collective-permute-start | bytes 393224 | tf_op jit(solution)/shard_map/ppermute | solution.py:202
  99.0 12.0 %all-gather.7.cloned.1.call-done = bf16[24,512,128]{2,1,0:T(8,128)(2,1)} async-done(((bf16[3,512,128]{2,1,0:T(8,128)(2,1)}), bf16[24,512,128]{2,1,0:T(8,128)(2,1)}) %all-gather.7.cloned.1.call-update) | async-done | bytes 3145744 | tf_op jit(solution)/shard_map/all_gather | solution.py:169
  111.0 0.0 collective-permute-done.3.theirs_ref
  111.0 0.0 copy-start.3
  111.0 0.0 copy-start.2
  111.0 3.9 %second_product.1 = bf16[4,2,128,256]{3,2,1,0:T(8,128)(2,1)} custom-call(s32[2]{0:T(128)} %pad_add_fusion.where_ref, bf16[128,512]{1,0:T(8,128)(2,1)S(1)} %fusion.mine_ref, bf16[128,512]{1,0:T(8,128)(2,1)S(1)} %collective-permute-done.3.theirs_ref, bf16[8,4,128,128]{3,2,1,0:T(8,128)(2,1)S(1)} %slice.23.near_ref, ...), custom_call_target="tpu_custom_call" | custom-call | flops 536870912 | bytes 5242880 | tf_op jit(solution)/shard_map/second_product/pallas_call | solution.py:126
  114.9 5.9 %all-to-all-start.2 = ((bf16[8,128,256]{2,1,0:T(8,128)(2,1)}), bf16[8,128,256]{2,1,0:T(8,128)(2,1)S(1)}, u32[]{:S(2)}, u32[]{:S(2)}) async-start(bf16[8,128,256]{2,1,0:T(8,128)(2,1)} %bitcast.16), calls=%async_computation.2 | async-start | bytes 1048576 | tf_op jit(solution)/shard_map/all_to_all | solution.py:204
  120.8 0.0 copy-done.3
  120.8 0.0 copy-done.2
  120.8 0.1 fusion.3
  120.9 6.8 %all-to-all-done.2 = bf16[8,128,256]{2,1,0:T(8,128)(2,1)S(1)} async-done(((bf16[8,128,256]{2,1,0:T(8,128)(2,1)}), bf16[8,128,256]{2,1,0:T(8,128)(2,1)S(1)}, u32[]{:S(2)}, u32[]{:S(2)}) %all-to-all-start.2) | async-done | bytes 524320 | tf_op jit(solution)/shard_map/all_to_all | solution.py:204
  127.7 0.1 convert_reduce_fusion
  127.7 0.8 fusion.1
  (3 shorter events, 0.0 us)
Async XLA Ops:
  6.5 31.5 %copy-start = (bf16[256,256]{1,0:T(8,128)(2,1)S(1)}, bf16[256,256]{1,0:T(8,128)(2,1)}, u32[]{:S(2)}) copy-start(bf16[256,256]{1,0:T(8,128)(2,1)} %param.6) | copy-start | bytes 393220
  6.5 60.2 %all-gather.5.cloned.1.call-start = ((), (), s32[]{:S(2)}) async-start(), calls=%async_computation.3 | async-start | bytes 3538944 | tf_op jit(solution)/shard_map/all_gather | solution.py:157
  8.4 102.6 %all-gather.7.cloned.1.call-start = ((), (), s32[]{:S(2)}) async-start(), calls=%async_computation.4 | async-start | bytes 3538944 | tf_op jit(solution)/shard_map/all_gather | solution.py:169
  8.4 18.9 %collective-permute-start.6 = (bf16[512,128]{1,0:T(8,128)(2,1)}, bf16[512,128]{1,0:T(8,128)(2,1)S(1)}, u32[]{:S(2)}, u32[]{:S(2)}) collective-permute-start(bf16[512,128]{1,0:T(8,128)(2,1)} %down_ref.1), channel_id=1, source_target_pairs={{0,128},{1,160},{16,144},{17,176},{32,129},{33,161},{48,145},{49,1... | collective-permute-start | bytes 393224 | tf_op jit(solution)/shard_map/ppermute | solution.py:168
  14.5 20.0 %collective-permute-start.5 = (bf16[512,128]{1,0:T(8,128)(2,1)}, bf16[512,128]{1,0:T(8,128)(2,1)S(1)}, u32[]{:S(2)}, u32[]{:S(2)}) collective-permute-start(bf16[512,128]{1,0:T(8,128)(2,1)} %down_ref.1), channel_id=1, source_target_pairs={{0,256},{1,288},{16,272},{17,304},{32,257},{33,289},{48,273},{49,3... | collective-permute-start | bytes 393224 | tf_op jit(solution)/shard_map/ppermute | solution.py:168
  23.6 12.8 %collective-permute-start.4 = (bf16[512,128]{1,0:T(8,128)(2,1)}, bf16[512,128]{1,0:T(8,128)(2,1)S(1)}, u32[]{:S(2)}, u32[]{:S(2)}) collective-permute-start(bf16[512,128]{1,0:T(8,128)(2,1)} %down_ref.1), channel_id=1, source_target_pairs={{0,384},{1,416},{16,400},{17,432},{32,385},{33,417},{48,401},{49,4... | collective-permute-start | bytes 393224 | tf_op jit(solution)/shard_map/ppermute | solution.py:168
  38.0 9.5 %collective-permute-start = (bf16[128,256]{1,0:T(8,128)(2,1)S(1)}, bf16[128,256]{1,0:T(8,128)(2,1)S(1)}, u32[]{:S(2)}, u32[]{:S(2)}) collective-permute-start(bf16[128,256]{1,0:T(8,128)(2,1)S(1)} %constant_dynamic-slice_fusion), channel_id=1, source_target_pairs={{0,0},{1,1},{2,2},{3,3},{4,128},{5,129},{6,130},{7,131},{8,256},{9... | collective-permute-start | bytes 196616 | tf_op jit(solution)/shard_map/ppermute | solution.py:181
  62.9 3.8 %collective-permute-start.1 = (bf16[4,2,128,256]{3,2,1,0:T(8,128)(2,1)S(1)}, bf16[4,2,128,256]{3,2,1,0:T(8,128)(2,1)S(1)}, u32[]{:S(2)}, u32[]{:S(2)}) collective-permute-start(bf16[4,2,128,256]{3,2,1,0:T(8,128)(2,1)S(1)} %bitcast.41), channel_id=1, source_target_pairs={{0,1},{1,0},{2,3},{3,2},{4,5},{5,4},{6,7},{7,6},{8,9},{9,8},{10,11... | collective-permute-start | bytes 1572872 | tf_op jit(solution)/shard_map/ppermute | solution.py:186
  72.0 24.7 %copy-start.1 = (f32[128,1024]{1,0:T(8,128)S(1)}, f32[128,1024]{1,0:T(8,128)}, u32[]{:S(2)}) copy-start(f32[128,1024]{1,0:T(8,128)} %get-tuple-element.11) | copy-start | bytes 1572868
  72.0 24.7 %all-to-all-start.1 = ((bf16[4,128,1024]{2,1,0:T(8,128)(2,1)}), bf16[4,128,1024]{2,1,0:T(8,128)(2,1)S(1)}, u32[]{:S(2)}, u32[]{:S(2)}) async-start(bf16[4,128,1024]{2,1,0:T(8,128)(2,1)} %get-tuple-element.13), calls=%async_computation.1 | async-start | bytes 2097152 | tf_op jit(solution)/shard_map/all_to_all | solution.py:194
  77.8 19.3 %collective-permute-start.2 = (bf16[2,2,4,128,128]{4,3,2,1,0:T(8,128)(2,1)}, bf16[2,2,4,128,128]{4,3,2,1,0:T(8,128)(2,1)S(1)}, u32[]{:S(2)}, u32[]{:S(2)}) collective-permute-start(bf16[2,2,4,128,128]{4,3,2,1,0:T(8,128)(2,1)} %dynamic-slice_bitcast_fusion), channel_id=1, source_target_pairs={{0,1},{1,0},{2,3},{3,2},{4,5},{5,4},{6,7},{7,6},{8,9},{9,8},{10,11... | collective-permute-start | bytes 1572872 | tf_op jit(solution)/shard_map/ppermute | solution.py:193
  97.1 13.9 %collective-permute-start.3 = (bf16[128,512]{1,0:T(8,128)(2,1)S(1)}, bf16[128,512]{1,0:T(8,128)(2,1)S(1)}, u32[]{:S(2)}, u32[]{:S(2)}) collective-permute-start(bf16[128,512]{1,0:T(8,128)(2,1)S(1)} %fusion.mine_ref), channel_id=1, source_target_pairs={{0,1},{1,0},{2,3},{3,2},{4,5},{5,4},{6,7},{7,6},{8,9},{9,8},{10,11... | collective-permute-start | bytes 393224 | tf_op jit(solution)/shard_map/ppermute | solution.py:202
  111.0 9.8 %copy-start.3 = (s32[2]{0:T(128)S(1)}, s32[2]{0:T(128)}, u32[]{:S(2)}) copy-start(s32[2]{0:T(128)} %param.10) | copy-start | bytes 28
  111.0 9.8 %copy-start.2 = (s32[256]{0:T(256)S(1)}, s32[256]{0:T(256)}, u32[]{:S(2)}) copy-start(s32[256]{0:T(256)} %param.11) | copy-start | bytes 3076
  114.9 12.7 %all-to-all-start.2 = ((bf16[8,128,256]{2,1,0:T(8,128)(2,1)}), bf16[8,128,256]{2,1,0:T(8,128)(2,1)S(1)}, u32[]{:S(2)}, u32[]{:S(2)}) async-start(bf16[8,128,256]{2,1,0:T(8,128)(2,1)} %bitcast.16), calls=%async_computation.2 | async-start | bytes 1048576 | tf_op jit(solution)/shard_map/all_to_all | solution.py:204
Sparse Core Ops, SparseCore 0:
  9.4 55.0 all-gather.4
  66.6 44.3 all-gather.6
